TPU v7x, 512 devices: a whole 4x8x8 slice. The times are simulated.
512 devices in a mesh: tile: 64 (over y, x, core), own: 8 (over z).
Axes of the slice: x: 4, y: 8, z: 8, core: 2. Of those that a mesh axis runs over, the one named last changes fastest.
Arguments:
- features: bfloat16 [2048, 8, 768], P('tile'), may hold values from -6 to 6
- cotangent: bfloat16 [2048, 8, 768], P('tile'), may hold values from -6 to 6
- depth_kernel: float32 [7, 7, 768], replicated, may hold values from -0.875 to 0.875
- ln_gain: float32 [768], replicated, may hold values from 0.1 to 1.9
- weight_up: bfloat16 [768, 3072], P('tile', 'own'), may hold values from -0.21875 to 0.21875
- bias_up: float32 [3072], P('own'), may hold values from -3 to 3
- weight_down: bfloat16 [3072, 768], P('own', 'tile'), may hold values from -0.109375 to 0.109375
- layer_scale: float32 [768], replicated, may hold values from 0.3 to 3
- tissue: int32 [256, 1], P('tile'), may hold values 0 or 1
- lengths: int32 [64], replicated, may hold values from 1 to 4, 128 in all
Outputs:
- block_out: bfloat16 [2048, 8, 768], P(('tile', 'own'))
- grad_features: bfloat16 [2048, 8, 768], P(('tile', 'own'))
- muon_up: float32 [768, 3072], P('tile', 'own')
- muon_down: float32 [3072, 768], P('own', 'tile')
Inputs may be any that keep to these rules, and one draw needn't show every extreme that they name: `lengths`: patch rows of slide in each strip; they sum to 128, and some strip has exactly 4.
All inputs are finite; a program needn't handle non-finite values. No bound on the sum of `tissue` on one device may be relied on, other than what follows from the above.
Results may differ from a plain program's by a relative error of at most 0.015.
Values may be sent and summed in bfloat16 or wider, within the bound.
A program may use at most 64 MiB of HBM per device.

v0:
```python
import jax
import jax.numpy as jnp
from jax import lax
from jax.sharding import PartitionSpec as P

KERNEL = 7
PATCH = 8
ITERS_NS = 2


INV_ROOT_TWO = 0.7071067811865476
INV_ROOT_TAU = 0.3989422804014327
NS_A = 3.4445
NS_B = -4.775
NS_C = 2.0315
EPS_NORM = 1e-06
HIGHEST_PREC = lax.Precision.HIGHEST


def padded_2(shard, sides, width):
    for axis, dim in sides:
        devices, length = (lax.axis_size(axis), shard.shape[dim])
        up = [(i, (i + 1) % devices) for i in range(devices - 1)]
        down = [(j, i) for i, j in up]
        last = lax.slice_in_dim(shard, length - width, length, axis=dim)
        initial = lax.slice_in_dim(shard, 0, width, axis=dim)
        before = lax.ppermute(last, axis, up)
        after = lax.ppermute(initial, axis, down)
        shard = jnp.concatenate([before, shard, after], axis=dim)
    return shard


def gelu_exact(hidden):
    return 0.5 * hidden * (1.0 + lax.erf(hidden * INV_ROOT_TWO))


def gelu_slope(hidden):
    return (
        0.5 * (1.0 + lax.erf(hidden * INV_ROOT_TWO))
        + hidden * jnp.exp(-0.5 * hidden * hidden) * INV_ROOT_TAU
    )


def depthwise(framed, kernel):
    margin = kernel.shape[0] // 2
    padded = jnp.pad(framed, ((0, 0), (margin, margin), (0, 0)))
    row_count = framed.shape[0] - 2 * margin
    col_count = framed.shape[1]
    totals = jnp.zeros((row_count, col_count, framed.shape[2]), jnp.float32)
    for row_tap in range(kernel.shape[0]):
        for col_tap in range(kernel.shape[1]):
            totals = (
                totals
                + kernel[row_tap, col_tap]
                * padded[row_tap : row_tap + row_count, col_tap : col_tap + col_count]
            )
    return totals


def layer_norm(mixed, ln_gain):
    average = jnp.mean(mixed, axis=-1, keepdims=True)
    shifted = mixed - average
    variance = jnp.mean(shifted * shifted, axis=-1, keepdims=True)
    inv_std = lax.rsqrt(variance + 1e-06)
    centred = shifted * inv_std
    return (centred, inv_std, (centred * ln_gain).astype(jnp.bfloat16))


def norm_back(grad_normed, centred, inv_std, ln_gain):
    scaled_grad = grad_normed * ln_gain
    first_mean = jnp.mean(scaled_grad, axis=-1, keepdims=True)
    second_mean = jnp.mean(scaled_grad * centred, axis=-1, keepdims=True)
    return inv_std * (scaled_grad - first_mean - centred * second_mean)


def branch_pass(normed_rows, grad_branch, up_full, bias_up, down_full):
    hidden = jnp.dot(normed_rows, up_full, preferred_element_type=jnp.float32) + bias_up
    activation = gelu_exact(hidden).astype(jnp.bfloat16)
    branch = jnp.dot(activation, down_full, preferred_element_type=jnp.float32)
    grad_act = lax.dot_general(
        grad_branch, down_full, (((1,), (1,)), ((), ())), preferred_element_type=jnp.float32
    )
    grad_hidden = (grad_act * gelu_slope(hidden)).astype(jnp.bfloat16)
    grad_normed = lax.dot_general(
        grad_hidden, up_full, (((1,), (1,)), ((), ())), preferred_element_type=jnp.float32
    )
    grad_up = lax.dot_general(
        normed_rows, grad_hidden, (((0,), (0,)), ((), ())), preferred_element_type=jnp.float32
    )
    grad_down_t = lax.dot_general(
        grad_branch, activation, (((0,), (0,)), ((), ())), preferred_element_type=jnp.float32
    )
    return (branch, grad_normed, grad_up, grad_down_t)


def ns_update(block, gram_matrix):
    polynomial = NS_B * gram_matrix + NS_C * jnp.dot(
        gram_matrix, gram_matrix, precision=HIGHEST_PREC, preferred_element_type=jnp.float32
    )
    return NS_A * block + jnp.dot(
        block, polynomial, precision=HIGHEST_PREC, preferred_element_type=jnp.float32
    )


def local_gram(block):
    return lax.dot_general(
        block,
        block,
        (((0,), (0,)), ((), ())),
        precision=HIGHEST_PREC,
        preferred_element_type=jnp.float32,
    )


def newton_schulz(gradient):
    scaled = gradient * lax.rsqrt(jnp.sum(gradient * gradient) + EPS_NORM)
    for sweep_index in range(ITERS_NS):
        scaled = ns_update(scaled, local_gram(scaled))
    return scaled


def rim_rows(source_field, live_rows, margin):
    tail_rows = lax.dynamic_slice_in_dim(source_field, live_rows - margin, margin, 0)
    return jnp.concatenate([source_field[:margin], tail_rows], 0)


def framed_rows(source_field, received, live_rows, margin):
    blank_rows = jnp.zeros((margin,) + source_field.shape[1:], source_field.dtype)
    framed = jnp.concatenate([received[:margin], source_field, blank_rows], 0)
    return lax.dynamic_update_slice_in_dim(framed, received[3 * margin :], live_rows + margin, 0)


def shards(
    features,
    cotangent,
    depth_kernel,
    ln_gain,
    weight_up,
    bias_up,
    weight_down,
    layer_scale,
    tissue,
    lengths,
):
    tile_rows, columns, channels = features.shape
    margin = KERNEL // 2
    tile_index = lax.axis_index("tile")
    own_index = lax.axis_index("own")
    own_count = lax.axis_size("own")
    tile_len = lengths[tile_index]
    live_rows = PATCH * tile_len
    row_live = jnp.arange(tile_rows) < live_rows
    patch_mask = jnp.repeat(jnp.repeat(tissue, PATCH, axis=0), PATCH, axis=1)
    keep_mask = jnp.where(row_live[:, None], patch_mask, 0).astype(jnp.float32)[:, :, None]
    inputs_live = jnp.where(row_live[:, None, None], features, jnp.zeros_like(features))
    received = padded_2(rim_rows(inputs_live, live_rows, margin), (("tile", 0),), margin)
    mixed = depthwise(
        framed_rows(inputs_live, received, live_rows, margin).astype(jnp.float32), depth_kernel
    )
    centred, inv_std, normed = layer_norm(mixed, ln_gain)
    grad_branch = (keep_mask * layer_scale * cotangent.astype(jnp.float32)).astype(jnp.bfloat16)
    up_full = lax.all_gather(weight_up, "tile", axis=0, tiled=True)
    down_full = lax.all_gather(weight_down, "tile", axis=1, tiled=True)
    normed_flat = normed.reshape(-1, channels)
    grad_branch_flat = grad_branch.reshape(-1, channels)
    branch, grad_normed, grad_up, grad_down = branch_pass(
        normed_flat, grad_branch_flat, up_full, bias_up, down_full
    )
    branch_rows = lax.psum_scatter(
        branch.reshape(tile_rows, columns, channels).astype(jnp.bfloat16),
        "own",
        scatter_dimension=0,
        tiled=True,
    ).astype(jnp.float32)
    grad_normed = (
        lax.psum(grad_normed.astype(jnp.bfloat16), "own")
        .astype(jnp.float32)
        .reshape(tile_rows, columns, channels)
    )
    own_share = tile_rows // own_count
    row_offset = own_index * own_share
    mine_live = lax.dynamic_slice_in_dim(row_live, row_offset, own_share, 0)[:, None, None]
    mine_keep = lax.dynamic_slice_in_dim(keep_mask, row_offset, own_share, 0)
    mine_inputs = lax.dynamic_slice_in_dim(features, row_offset, own_share, 0).astype(jnp.float32)
    block_out = jnp.where(
        mine_live, mine_inputs + mine_keep * layer_scale * branch_rows, 0.0
    ).astype(jnp.bfloat16)
    grad_mixed = norm_back(grad_normed, centred, inv_std, ln_gain)
    grad_mixed = jnp.where(row_live[:, None, None], grad_mixed, 0.0)
    received_grad = padded_2(
        rim_rows(grad_mixed, live_rows, margin).astype(jnp.bfloat16), (("tile", 0),), margin
    ).astype(jnp.float32)
    spread = depthwise(
        framed_rows(grad_mixed, received_grad, live_rows, margin), depth_kernel[::-1, ::-1]
    )
    mine_cot = lax.dynamic_slice_in_dim(cotangent, row_offset, own_share, 0).astype(jnp.float32)
    grad_features = jnp.where(
        mine_live, mine_cot + lax.dynamic_slice_in_dim(spread, row_offset, own_share, 0), 0.0
    ).astype(jnp.bfloat16)
    whole_up, whole_down = lax.psum((grad_up, grad_down), "tile")
    ortho_up = newton_schulz(whole_up)
    ortho_down = newton_schulz(whole_down)
    rows_each = channels // lax.axis_size("tile")
    muon_up = lax.dynamic_slice_in_dim(ortho_up, tile_index * rows_each, rows_each, 0)
    muon_down = lax.dynamic_slice_in_dim(ortho_down, tile_index * rows_each, rows_each, 0).T
    return (block_out, grad_features, muon_up, muon_down)


def solution(mesh):
    in_specs = (
        P("tile", None, None),
        P("tile", None, None),
        P(),
        P(),
        P("tile", "own"),
        P("own"),
        P("own", "tile"),
        P(),
        P("tile", None),
        P(),
    )
    out_specs = (
        P(("tile", "own"), None, None),
        P(("tile", "own"), None, None),
        P("tile", "own"),
        P("own", "tile"),
    )
    return jax.shard_map(shards, mesh=mesh, in_specs=in_specs, out_specs=out_specs, check_vma=False)
```

profile of v0, /device:TPU:1, one launch (start us, length us, event | category | flops | bytes accessed | tf_op | source)
XLA Modules:
  0.0 467.4 jit_solution(9791858157561742824)
XLA Ops:
  8.1 1.2 dynamic_slice.28
  10.0 1.1 broadcast_select_fusion
  11.1 8.8 %collective-permute-start.1 = (bf16[3,8,768]{2,1,0:T(8,128)(2,1)S(1)}, bf16[3,8,768]{2,1,0:T(8,128)(2,1)S(1)}, u32[]{:S(2)}, u32[]{:S(2)}) collective-permute-start(bf16[3,8,768]{2,1,0:T(8,128)(2,1)S(1)} %get-tuple-element.65), channel_id=1, source_target_pairs={{8,0},{16,8},{24,16},{32,24},{40,32},{48,40},{56,48},{64,56},{72,6... | collective-permute-start | bytes 110600 | tf_op jit(solution)/shard_map/ppermute | solution.py:28
  19.9 1.9 collective-permute-start
  21.8 1.1 slice_reduce_fusion.46
  23.0 1.4 slice_reduce_fusion.48
  24.6 2.0 slice_reduce_fusion.47
  26.9 48.0 %all-gather = bf16[64,12,384]{2,1,0:T(8,128)(2,1)S(1)} all-gather(bf16[1,12,384]{2,1,0:T(8,128)(2,1)S(1)} %bitcast.58), channel_id=1, replica_groups=mesh['tile'=64,'own'=8] {'tile'}, dimensions={0}, use_global_device_ids=true | all-gather | bytes 599040 | tf_op jit(solution)/shard_map/all_gather | solution.py:162
  74.9 49.7 %all-gather.1 = bf16[64,12,384]{2,1,0:T(8,128)(2,1)S(1)} all-gather(bf16[1,12,384]{2,1,0:T(8,128)(2,1)S(1)} %bitcast.59), channel_id=1, replica_groups=mesh['tile'=64,'own'=8] {'tile'}, dimensions={0}, use_global_device_ids=true | all-gather | bytes 599040 | tf_op jit(solution)/shard_map/all_gather | solution.py:163
  124.6 0.6 constant_dynamic-slice_fusion.1
  125.2 0.6 dynamic_slice.29
  126.9 7.0 %fusion.215 = (f32[32,8]{1,0:T(8,128)S(1)}, f32[32,8,768]{2,1,0:T(8,128)S(1)}) fusion(f32[768]{0:T(1024)S(1)} %get-tuple-element.51, f32[768]{0:T(1024)S(1)} %get-tuple-element.52, f32[768]{0:T(1024)S(1)} %get-tuple-element.5, f32[38,8,768]{2,1,0:T(8,128)S(1)} %convert_element_type.61, f32[768]{0:T(1024)S(1)} %get-tuple-element.6, ...), kind=kLoop, calls=%fused_computation.408 | loop fusion | flops 19267328 | bytes 7420928 | tf_op jit(solution)/shard_map/reduce_sum | solution.py:61
  133.9 0.2 multiply_reduce_fusion.2
  134.1 0.4 convolution_add_fusion.2
  134.6 0.3 copy-done.3
  134.8 0.5 fusion.5
  135.3 1.1 convolution_convert_fusion
  136.5 1.2 fusion.4
  137.7 1.5 fusion.211
  139.2 0.3 all-reduce.8.cloned.1.call-start
  139.5 72.0 %all-reduce.6.cloned.1.call-done = bf16[256,768]{1,0:T(8,128)(2,1)} async-done(((bf16[256,768]{1,0:T(8,128)(2,1)}), bf16[256,768]{1,0:T(8,128)(2,1)}) %all-reduce.6.cloned.1.call-update) | async-done | bytes 393232 | tf_op jit(solution)/shard_map/psum | solution.py:176
  211.5 1.3 fusion.18
  212.9 0.2 fusion.19
  213.1 0.3 fusion.17
  213.5 8.0 %collective-permute-start.2 = (bf16[3,8,768]{2,1,0:T(8,128)(2,1)S(1)}, bf16[3,8,768]{2,1,0:T(8,128)(2,1)S(1)}, u32[]{:S(2)}, u32[]{:S(2)}) collective-permute-start(bf16[3,8,768]{2,1,0:T(8,128)(2,1)S(1)} %get-tuple-element.63), channel_id=1, source_target_pairs={{0,8},{8,16},{16,24},{24,32},{32,40},{40,48},{48,56},{56,64},{64,7... | collective-permute-start | bytes 110600 | tf_op jit(solution)/shard_map/ppermute | solution.py:27
  221.5 1.9 collective-permute-start.3
  223.4 1.5 fusion.200
  225.0 1.8 collective-permute-done.3
  227.3 1.5 fusion.189
  229.2 6.1 %fusion.171 = f32[32,8,768]{2,1,0:T(8,128)} fusion(f32[38,8,768]{2,1,0:T(8,128)S(1)} %convert_dynamic-update-slice_fusion, f32[768]{0:T(1024)S(1)} %copy-done.18, f32[768]{0:T(1024)S(1)} %copy-done.20, f32[768]{0:T(1024)S(1)} %copy-done.24, f32[768]{0:T(1024)S(1)} %copy-done.26, f32[768]{0:T(1024)S(1)} %copy-done.28, f32[768]{0:T(1024)S(1)} %copy-done.30, ...), kind=kLoop, calls=%fused_computation.270 | loop fusion | flops 16711680 | bytes 6608896 | tf_op jit(solution)/shard_map/add | solution.py:53
  235.3 18.0 %reduce-scatter.2.cloned.1.call-done = bf16[4,8,768]{2,1,0:T(8,128)(2,1)} async-done(((bf16[32,8,768]{2,1,0:T(8,128)(2,1)}), bf16[4,8,768]{2,1,0:T(8,128)(2,1)}) %reduce-scatter.2.cloned.1.call-update) | async-done | bytes 49168 | tf_op jit(solution)/shard_map/reduce_scatter | solution.py:169
  253.2 1.8 fusion.206
  255.0 167.9 %all-reduce.8.cloned.1.call-done = (f32[768,384]{1,0:T(8,128)}, f32[768,384]{1,0:T(8,128)}) async-done(((f32[768,384]{1,0:T(8,128)}, f32[768,384]{1,0:T(8,128)}), (f32[768,384]{1,0:T(8,128)}, f32[768,384]{1,0:T(8,128)})) %all-reduce.8.cloned.1.call-update) | async-done | bytes 2359312 | tf_op jit(solution)/shard_map/psum | solution.py:200
  423.0 2.6 multiply_reduce_fusion
  427.0 2.1 fusion.6
  429.1 1.3 fusion.2
  430.4 2.3 convolution_add_fusion
  432.7 2.0 fusion.220
  434.8 1.3 fusion.3
  436.0 11.1 %fusion.221 = f32[768,384]{1,0:T(8,128)S(1)} fusion(f32[768,384]{1,0:T(8,128)S(1)} %convolution_add_fusion, f32[384,384]{1,0:T(8,128)S(1)} %fusion.3), kind=kOutput, calls=%fused_computation.413 | convolution fusion | flops 1358954496 | bytes 2949120 | tf_op jit(solution)/shard_map/dot_general | solution.py:100
  447.1 2.1 fusion.9
  449.2 1.3 fusion
  450.5 2.3 convolution_add_fusion.1
  452.8 2.0 fusion.218
  454.9 1.3 fusion.1
  456.2 2.3 fusion.219
  458.5 0.6 fusion.214
  459.1 0.6 dynamic-slice_add_fusion.2
  (208 shorter events, 1.6 us)
Async XLA Ops:
  8.0 66.9 %copy-start.86 = (bf16[384,12]{0,1:T(8,128)(2,1)S(1)}, bf16[384,12]{0,1:T(8,128)(2,1)}, u32[]{:S(2)}) copy-start(bf16[384,12]{0,1:T(8,128)(2,1)} %param.16) | copy-start | bytes 27652
  8.0 203.5 %all-reduce.6.cloned.1.call-start = ((), (), s32[]{:S(2)}) async-start(), calls=%async_computation.2 | async-start | bytes 786432 | tf_op jit(solution)/shard_map/psum | solution.py:176
  11.1 115.2 %collective-permute-start.1 = (bf16[3,8,768]{2,1,0:T(8,128)(2,1)S(1)}, bf16[3,8,768]{2,1,0:T(8,128)(2,1)S(1)}, u32[]{:S(2)}, u32[]{:S(2)}) collective-permute-start(bf16[3,8,768]{2,1,0:T(8,128)(2,1)S(1)} %get-tuple-element.65), channel_id=1, source_target_pairs={{8,0},{16,8},{24,16},{32,24},{40,32},{48,40},{56,48},{64,56},{72,6... | collective-permute-start | bytes 110600 | tf_op jit(solution)/shard_map/ppermute | solution.py:28
  19.9 106.3 %collective-permute-start = (bf16[3,8,768]{2,1,0:T(8,128)(2,1)S(1)}, bf16[3,8,768]{2,1,0:T(8,128)(2,1)S(1)}, u32[]{:S(2)}, u32[]{:S(2)}) collective-permute-start(bf16[3,8,768]{2,1,0:T(8,128)(2,1)S(1)} %get-tuple-element.66), channel_id=1, source_target_pairs={{0,8},{8,16},{16,24},{24,32},{32,40},{40,48},{48,56},{56,64},{64,7... | collective-permute-start | bytes 110600 | tf_op jit(solution)/shard_map/ppermute | solution.py:27
  22.9 103.5 %copy-start.7 = (f32[768]{0:T(1024)}, f32[768]{0:T(1024)S(1)}, u32[]{:S(2)}) copy-start(f32[768]{0:T(1024)S(1)} %get-tuple-element.43) | copy-start | bytes 9220
  22.9 103.5 %copy-start.9 = (f32[768]{0:T(1024)}, f32[768]{0:T(1024)S(1)}, u32[]{:S(2)}) copy-start(f32[768]{0:T(1024)S(1)} %get-tuple-element.44) | copy-start | bytes 9220
  23.0 103.5 %copy-start.11 = (f32[768]{0:T(1024)}, f32[768]{0:T(1024)S(1)}, u32[]{:S(2)}) copy-start(f32[768]{0:T(1024)S(1)} %get-tuple-element.45) | copy-start | bytes 9220
  23.0 103.5 %copy-start.13 = (f32[768]{0:T(1024)}, f32[768]{0:T(1024)S(1)}, u32[]{:S(2)}) copy-start(f32[768]{0:T(1024)S(1)} %get-tuple-element.46) | copy-start | bytes 9220
  23.0 103.5 %copy-start.15 = (f32[768]{0:T(1024)}, f32[768]{0:T(1024)S(1)}, u32[]{:S(2)}) copy-start(f32[768]{0:T(1024)S(1)} %get-tuple-element.47) | copy-start | bytes 9220
  23.0 103.5 %copy-start.17 = (f32[768]{0:T(1024)}, f32[768]{0:T(1024)S(1)}, u32[]{:S(2)}) copy-start(f32[768]{0:T(1024)S(1)} %get-tuple-element.51) | copy-start | bytes 9220
  23.0 103.5 %copy-start.19 = (f32[768]{0:T(1024)}, f32[768]{0:T(1024)S(1)}, u32[]{:S(2)}) copy-start(f32[768]{0:T(1024)S(1)} %get-tuple-element.52) | copy-start | bytes 9220
  23.0 103.5 %copy-start.21 = (f32[768]{0:T(1024)}, f32[768]{0:T(1024)S(1)}, u32[]{:S(2)}) copy-start(f32[768]{0:T(1024)S(1)} %get-tuple-element.48) | copy-start | bytes 9220
  24.4 102.1 %copy-start.23 = (f32[768]{0:T(1024)}, f32[768]{0:T(1024)S(1)}, u32[]{:S(2)}) copy-start(f32[768]{0:T(1024)S(1)} %get-tuple-element.5) | copy-start | bytes 9220
  24.4 102.1 %copy-start.25 = (f32[768]{0:T(1024)}, f32[768]{0:T(1024)S(1)}, u32[]{:S(2)}) copy-start(f32[768]{0:T(1024)S(1)} %get-tuple-element.6) | copy-start | bytes 9220
  24.4 102.1 %copy-start.27 = (f32[768]{0:T(1024)}, f32[768]{0:T(1024)S(1)}, u32[]{:S(2)}) copy-start(f32[768]{0:T(1024)S(1)} %get-tuple-element.7) | copy-start | bytes 9220
  24.4 102.1 %copy-start.29 = (f32[768]{0:T(1024)}, f32[768]{0:T(1024)S(1)}, u32[]{:S(2)}) copy-start(f32[768]{0:T(1024)S(1)} %get-tuple-element.8) | copy-start | bytes 9220
  24.4 102.1 %copy-start.31 = (f32[768]{0:T(1024)}, f32[768]{0:T(1024)S(1)}, u32[]{:S(2)}) copy-start(f32[768]{0:T(1024)S(1)} %get-tuple-element.9) | copy-start | bytes 9220
  24.5 102.1 %copy-start.33 = (f32[768]{0:T(1024)}, f32[768]{0:T(1024)S(1)}, u32[]{:S(2)}) copy-start(f32[768]{0:T(1024)S(1)} %get-tuple-element.10) | copy-start | bytes 9220
  24.5 102.1 %copy-start.35 = (f32[768]{0:T(1024)}, f32[768]{0:T(1024)S(1)}, u32[]{:S(2)}) copy-start(f32[768]{0:T(1024)S(1)} %get-tuple-element.11) | copy-start | bytes 9220
  24.5 102.1 %copy-start.37 = (f32[768]{0:T(1024)}, f32[768]{0:T(1024)S(1)}, u32[]{:S(2)}) copy-start(f32[768]{0:T(1024)S(1)} %get-tuple-element.12) | copy-start | bytes 9220
  24.5 102.1 %copy-start.39 = (f32[768]{0:T(1024)}, f32[768]{0:T(1024)S(1)}, u32[]{:S(2)}) copy-start(f32[768]{0:T(1024)S(1)} %get-tuple-element.13) | copy-start | bytes 9220
  24.5 102.1 %copy-start.41 = (f32[768]{0:T(1024)}, f32[768]{0:T(1024)S(1)}, u32[]{:S(2)}) copy-start(f32[768]{0:T(1024)S(1)} %get-tuple-element.14) | copy-start | bytes 9220
  24.5 102.1 %copy-start.43 = (f32[768]{0:T(1024)}, f32[768]{0:T(1024)S(1)}, u32[]{:S(2)}) copy-start(f32[768]{0:T(1024)S(1)} %get-tuple-element.15) | copy-start | bytes 9220
  24.5 102.1 %copy-start.45 = (f32[768]{0:T(1024)}, f32[768]{0:T(1024)S(1)}, u32[]{:S(2)}) copy-start(f32[768]{0:T(1024)S(1)} %get-tuple-element.16) | copy-start | bytes 9220
  24.5 102.1 %copy-start.47 = (f32[768]{0:T(1024)}, f32[768]{0:T(1024)S(1)}, u32[]{:S(2)}) copy-start(f32[768]{0:T(1024)S(1)} %get-tuple-element.17) | copy-start | bytes 9220
  24.5 102.1 %copy-start.49 = (f32[768]{0:T(1024)}, f32[768]{0:T(1024)S(1)}, u32[]{:S(2)}) copy-start(f32[768]{0:T(1024)S(1)} %get-tuple-element.18) | copy-start | bytes 9220
  24.5 102.1 %copy-start.51 = (f32[768]{0:T(1024)}, f32[768]{0:T(1024)S(1)}, u32[]{:S(2)}) copy-start(f32[768]{0:T(1024)S(1)} %get-tuple-element.19) | copy-start | bytes 9220
  24.6 102.1 %copy-start.53 = (f32[768]{0:T(1024)}, f32[768]{0:T(1024)S(1)}, u32[]{:S(2)}) copy-start(f32[768]{0:T(1024)S(1)} %get-tuple-element.20) | copy-start | bytes 9220
  24.6 102.1 %copy-start.55 = (f32[768]{0:T(1024)}, f32[768]{0:T(1024)S(1)}, u32[]{:S(2)}) copy-start(f32[768]{0:T(1024)S(1)} %get-tuple-element.21) | copy-start | bytes 9220
  24.6 102.1 %copy-start.57 = (f32[768]{0:T(1024)}, f32[768]{0:T(1024)S(1)}, u32[]{:S(2)}) copy-start(f32[768]{0:T(1024)S(1)} %get-tuple-element.22) | copy-start | bytes 9220
  26.6 100.1 %copy-start.5 = (f32[768]{0:T(1024)}, f32[768]{0:T(1024)S(1)}, u32[]{:S(2)}) copy-start(f32[768]{0:T(1024)S(1)} %get-tuple-element.23) | copy-start | bytes 9220
  26.6 100.1 %copy-start.59 = (f32[768]{0:T(1024)}, f32[768]{0:T(1024)S(1)}, u32[]{:S(2)}) copy-start(f32[768]{0:T(1024)S(1)} %get-tuple-element.24) | copy-start | bytes 9220
  26.6 100.1 %copy-start.61 = (f32[768]{0:T(1024)}, f32[768]{0:T(1024)S(1)}, u32[]{:S(2)}) copy-start(f32[768]{0:T(1024)S(1)} %get-tuple-element.25) | copy-start | bytes 9220
  26.6 100.2 %copy-start.63 = (f32[768]{0:T(1024)}, f32[768]{0:T(1024)S(1)}, u32[]{:S(2)}) copy-start(f32[768]{0:T(1024)S(1)} %get-tuple-element.26) | copy-start | bytes 9220
  26.6 100.2 %copy-start.65 = (f32[768]{0:T(1024)}, f32[768]{0:T(1024)S(1)}, u32[]{:S(2)}) copy-start(f32[768]{0:T(1024)S(1)} %get-tuple-element.27) | copy-start | bytes 9220
  26.6 100.2 %copy-start.67 = (f32[768]{0:T(1024)}, f32[768]{0:T(1024)S(1)}, u32[]{:S(2)}) copy-start(f32[768]{0:T(1024)S(1)} %get-tuple-element.28) | copy-start | bytes 9220
  26.6 100.2 %copy-start.69 = (f32[768]{0:T(1024)}, f32[768]{0:T(1024)S(1)}, u32[]{:S(2)}) copy-start(f32[768]{0:T(1024)S(1)} %get-tuple-element.29) | copy-start | bytes 9220
  26.6 100.2 %copy-start.71 = (f32[768]{0:T(1024)}, f32[768]{0:T(1024)S(1)}, u32[]{:S(2)}) copy-start(f32[768]{0:T(1024)S(1)} %get-tuple-element.30) | copy-start | bytes 9220
  26.6 100.2 %copy-start.73 = (f32[768]{0:T(1024)}, f32[768]{0:T(1024)S(1)}, u32[]{:S(2)}) copy-start(f32[768]{0:T(1024)S(1)} %get-tuple-element.31) | copy-start | bytes 9220
  26.6 100.2 %copy-start.75 = (f32[768]{0:T(1024)}, f32[768]{0:T(1024)S(1)}, u32[]{:S(2)}) copy-start(f32[768]{0:T(1024)S(1)} %get-tuple-element.32) | copy-start | bytes 9220
  26.6 100.2 %copy-start.77 = (f32[768]{0:T(1024)}, f32[768]{0:T(1024)S(1)}, u32[]{:S(2)}) copy-start(f32[768]{0:T(1024)S(1)} %get-tuple-element.33) | copy-start | bytes 9220
  26.7 100.2 %copy-start.79 = (f32[768]{0:T(1024)}, f32[768]{0:T(1024)S(1)}, u32[]{:S(2)}) copy-start(f32[768]{0:T(1024)S(1)} %get-tuple-element.34) | copy-start | bytes 9220
  26.7 100.2 %copy-start.81 = (f32[768]{0:T(1024)}, f32[768]{0:T(1024)S(1)}, u32[]{:S(2)}) copy-start(f32[768]{0:T(1024)S(1)} %get-tuple-element.35) | copy-start | bytes 9220
  136.5 116.8 %reduce-scatter.2.cloned.1.call-start = ((), (), s32[]{:S(2)}) async-start(), calls=%async_computation.1 | async-start | bytes 442368 | tf_op jit(solution)/shard_map/reduce_scatter | solution.py:169
  139.2 283.7 %all-reduce.8.cloned.1.call-start = ((), (), s32[]{:S(2)}) async-start(), calls=%async_computation.3 | async-start | bytes 4718592 | tf_op jit(solution)/shard_map/psum | solution.py:200
  213.5 11.5 %collective-permute-start.2 = (bf16[3,8,768]{2,1,0:T(8,128)(2,1)S(1)}, bf16[3,8,768]{2,1,0:T(8,128)(2,1)S(1)}, u32[]{:S(2)}, u32[]{:S(2)}) collective-permute-start(bf16[3,8,768]{2,1,0:T(8,128)(2,1)S(1)} %get-tuple-element.63), channel_id=1, source_target_pairs={{0,8},{8,16},{16,24},{24,32},{32,40},{40,48},{48,56},{56,64},{64,7... | collective-permute-start | bytes 110600 | tf_op jit(solution)/shard_map/ppermute | solution.py:27
  221.5 5.3 %collective-permute-start.3 = (bf16[3,8,768]{2,1,0:T(8,128)(2,1)S(1)}, bf16[3,8,768]{2,1,0:T(8,128)(2,1)S(1)}, u32[]{:S(2)}, u32[]{:S(2)}) collective-permute-start(bf16[3,8,768]{2,1,0:T(8,128)(2,1)S(1)} %get-tuple-element.64), channel_id=1, source_target_pairs={{8,0},{16,8},{24,16},{32,24},{40,32},{48,40},{56,48},{64,56},{72,6... | collective-permute-start | bytes 110600 | tf_op jit(solution)/shard_map/ppermute | solution.py:28
  229.2 24.1 %copy-start.6 = (f32[768]{0:T(1024)S(1)}, f32[768]{0:T(1024)}, u32[]{:S(2)}) copy-start(f32[768]{0:T(1024)} %copy-done.5) | copy-start | bytes 9220
  (48 other events, 164.7 us)
Sparse Core Ops, SparseCore 0:
  136.6 74.8 all-reduce.5
  214.5 38.6 reduce-scatter.1
Sparse Core Ops, SparseCore 1:
  225.0 197.9 all-reduce.7
where the time goes:
time: 474 us; the launch traced here: 467 us
  waiting for transfers between devices  260 us (55%)
  blocking collectives  97.7 us (21%)
  matrix products  37.6 us (8%)
  other arithmetic  23.7 us (5%)
  starting transfers between devices  21 us (4%)
  between operations  19.3 us (4%)
  local copies, waits for them, and re-layouts  8.22 us (2%)
    psum x1, waiting for transfers between devices, shards(): whole_up, whole_down = lax.psum((grad_up, grad_down), 'tile')  168 us
    psum x1, waiting for transfers between devices, shards(): lax.psum(grad_normed.astype(jnp.bfloat16), 'own').astype(jnp.float32)  72 us
    all_gather x1, blocking collectives, shards(): down_full = lax.all_gather(weight_down, 'tile', axis=1, tiled=True)  49.7 us
    all_gather x1, blocking collectives, shards(): up_full = lax.all_gather(weight_up, 'tile', axis=0, tiled=True)  48 us
    dot_general x4, matrix products, ns_update(): jnp.dot(block, polynomial, precision=HIGHEST_PREC, preferred_element_type...  18.1 us
    reduce_scatter x1, waiting for transfers between devices, shards(): lax.psum_scatter(branch.reshape(tile_rows, columns, channels).astype(jnp....  18 us
    ppermute x2, starting transfers between devices, padded_2(): after = lax.ppermute(initial, axis, down)  10.7 us
    ppermute x2, starting transfers between devices, padded_2(): before = lax.ppermute(last, axis, up)  9.95 us
  transfers between devices with their start and end apart: 7, of which 4 were waited for; matrix products, arithmetic and copies ran while one was open for 5% of the time, Pallas kernels for 0%

commit v1 on v0

v1 whole, which is shorter than its diff:
```python
import jax
import jax.numpy as jnp
from jax import lax
from jax.experimental import pallas as pl
from jax.experimental.pallas import tpu as pltpu
from jax.sharding import PartitionSpec as P

MESH = pl.DeviceIdType.MESH
F32 = jnp.float32
BF16 = jnp.bfloat16

NY, NX, NZ = 8, 4, 8
NT = NY * NX * 2
D = 768
HID = 384
TOK = 256
CH = D // 128
RB = 24
OWN_TOK = 32

INV_ROOT_TWO = 0.7071067811865476
INV_ROOT_TAU = 0.3989422804014327
NS_A = 3.4445
NS_B = -4.775
NS_C = 2.0315
EPS_NORM = 1e-06
HIGH = lax.Precision.HIGH


def f32dot(a, b, dims=(((1,), (0,)), ((), ()))):
    return lax.dot_general(a, b, dims, precision=HIGH, preferred_element_type=F32)


def bdot(a, b, dims=(((1,), (0,)), ((), ()))):
    return lax.dot_general(a, b, dims, preferred_element_type=F32)


NT_DIMS = (((1,), (1,)), ((), ()))
TN_DIMS = (((0,), (0,)), ((), ()))


def body(
    lens, tissue, feat, cot, dk, gain, wu, bias, wd, scale,
    out_ref, gout_ref, mu_ref, md_ref,
    pieces, piece_in, t24, wg, wm, fx, rim, halo, frame, mixed, inv_s, left, right,
    zs, zr, bs, br, gs, grv, gf, gb, rx, gx, ty, ry, grow, ga, gm16, hg, nb, ct, chd, frame2, xo,
    ss, rs,
):
    t = lax.axis_index("tile")
    o = lax.axis_index("own")
    c = lax.rem(t, 2)
    chip = t // 2
    x = lax.rem(chip, NX)
    y = chip // NX
    sib = t + 1 - 2 * c

    def tile_at(yy, xx):
        return (yy * NX + xx) * 2 + c

    counter = [0]
    sent = []

    def sem_ids(n):
        first = counter[0]
        counter[0] += n
        return first

    def copy(src, dst, sem, dev):
        return pltpu.make_async_remote_copy(
            src_ref=src, dst_ref=dst, send_sem=ss.at[sem], recv_sem=rs.at[sem],
            device_id=dev, device_id_type=MESH,
        )

    def send(src, dst, sem, dev):
        cp = copy(src, dst, sem, dev)
        cp.start()
        sent.append(cp)

    def arrived(dst, sem):
        copy(dst, dst, sem, (t, o)).wait_recv()

    bar = pltpu.get_barrier_semaphore()

    def greet(dev):
        pl.semaphore_signal(bar, inc=1, device_id=dev, device_id_type=MESH)

    up_t = lax.rem(t + 1, NT)
    dn_t = lax.rem(t + NT - 1, NT)
    greet((sib, o))
    for k in range(1, NY):
        greet((tile_at(lax.rem(y + k, NY), x), o))
    for k in range(1, NX):
        greet((tile_at(y, lax.rem(x + k, NX)), o))
    for k in range(1, NZ):
        greet((t, lax.rem(o + k, NZ)))
    greet((up_t, o))
    greet((dn_t, o))
    first_own = o == 0
    odd_own = lax.rem(o, 2) == 1

    @pl.when(first_own)
    def _():
        for q in range(4):
            greet((dn_t, 2 * q + 1))

    @pl.when(odd_own)
    def _():
        greet((up_t, 0))

    length = lens[t]

    pieces[0] = wu[...]
    pieces[1] = wd[...]
    rim[0] = feat[0:24, :].astype(F32).astype(BF16)
    tail = feat[0:64, :].astype(F32)[40:64]
    for q in range(1, 4):
        tail = jnp.where(length == q + 1, feat[64 * q : 64 * q + 64, :].astype(F32)[40:64], tail)
    rim[1] = tail.astype(BF16)

    expected = 1 + (NY - 1) + (NX - 1) + (NZ - 1) + 2
    pl.semaphore_wait(bar, expected + 4 * ((NZ - o) // NZ) + lax.rem(o, 2))

    s_piece = sem_ids(1)
    send(pieces.at[1 - c], piece_in, s_piece, (sib, o))
    s_halo = sem_ids(2)
    send(rim.at[1], halo.at[0], s_halo, (up_t, o))
    send(rim.at[0], halo.at[1], s_halo + 1, (dn_t, o))

    frame[...] = jnp.zeros_like(frame)
    for q in range(4):
        rows = slice(64 * q, 64 * q + 64)
        live = length > q
        keep = jnp.where(live, tissue[q, 0], 0).astype(F32)
        f = feat[rows, :].astype(F32)
        if q:
            f = jnp.where(live, f, 0.0)
        for ch in range(CH):
            frame[ch, 3 + 8 * q : 11 + 8 * q, 3:11, :] = f[:, 128 * ch : 128 * ch + 128].reshape(8, 8, 128)
        left[1, rows, :] = ((keep * scale[...]) * cot[rows, :].astype(F32)).astype(BF16)

    arrived(piece_in, s_piece)
    mine = pieces[c].astype(F32)
    other = piece_in[...].astype(F32)
    t24[0:12, :] = jnp.where(c == 0, mine, other)
    t24[12:24, :] = jnp.where(c == 0, other, mine)
    wg[c, y, x] = t24[...].astype(BF16)

    def gather_y(buf, s0):
        for k in range(1, NY):
            send(buf.at[y, x], buf.at[y, x], s0 + k - 1, (tile_at(lax.rem(y + k, NY), x), o))

    def gather_y_wait(buf, s0):
        for k in range(1, NY):
            arrived(buf.at[lax.rem(y + NY - k, NY), x], s0 + k - 1)

    def gather_x(buf, s0):
        for k in range(1, NX):
            send(buf.at[:, x], buf.at[:, x], s0 + k - 1, (tile_at(y, lax.rem(x + k, NX)), o))

    s_wy = sem_ids(NY - 1)
    s_wx = sem_ids(NX - 1)
    s_ws = sem_ids(NX)
    wg_c = wg.at[c]
    gather_y(wg_c, s_wy)

    arrived(halo.at[0], s_halo)
    arrived(halo.at[1], s_halo + 1)
    before = jnp.where(t > 0, halo[0].astype(F32), 0.0)
    after = jnp.where(t < NT - 1, halo[1].astype(F32), 0.0)
    for ch in range(CH):
        lanes = slice(128 * ch, 128 * ch + 128)
        frame[ch, 0:3, 3:11, :] = before[:, lanes].reshape(3, 8, 128)
        nxt = after[:, lanes].reshape(3, 8, 128)
        for q in range(1, 4):
            old = frame[ch, 3 + 8 * q : 6 + 8 * q, 3:11, :]
            frame[ch, 3 + 8 * q : 6 + 8 * q, 3:11, :] = jnp.where(length == q, nxt, old)
        frame[ch, 35:38, 3:11, :] = jnp.where(length == 4, nxt, 0.0)

    def conv_half(h):
        def chunk(ch, _):
            lanes = pl.ds(pl.multiple_of(ch * 128, 128), 128)
            acc = jnp.zeros((16, 8, 128), F32)
            for i in range(7):
                for j in range(7):
                    w = dk[i, j : j + 1, lanes].reshape(1, 1, 128)
                    acc = acc + w * frame[ch, 16 * h + i : 16 * h + i + 16, j : j + 8, :]
            mixed[128 * h : 128 * h + 128, lanes] = acc.reshape(128, 128)
            return 0

        lax.fori_loop(0, CH, chunk, 0)

    conv_half(0)
    gather_y_wait(wg_c, s_wy)
    gather_x(wg_c, s_wx)
    send(wg_c.at[:, x], wg_c.at[:, x], s_ws, (sib, o))
    conv_half(1)

    for q in range(4):
        rows = slice(64 * q, 64 * q + 64)
        m = mixed[rows, :]
        shifted = m - jnp.sum(m, axis=-1, keepdims=True) * (1.0 / D)
        var = jnp.sum(shifted * shifted, axis=-1, keepdims=True) * (1.0 / D)
        inv = lax.rsqrt(var + 1e-06)
        centred = shifted * inv
        mixed[rows, :] = centred
        inv_s[rows, :] = inv
        left[0, rows, :] = (centred * gain[...]).astype(BF16)

    for k in range(1, NX):
        col = lax.rem(x + NX - k, NX)
        arrived(wg_c.at[:, col], s_wx + k - 1)
        send(wg_c.at[:, col], wg_c.at[:, col], s_ws + k, (sib, o))
    wm[c] = wg[c].astype(F32).reshape(D, HID).astype(BF16)
    wg_o = wg.at[1 - c]
    for k in range(NX):
        arrived(wg_o.at[:, lax.rem(x + NX - k, NX)], s_ws + k)
    wm[1 - c] = wg[1 - c].astype(F32).reshape(D, HID).astype(BF16)

    up_w = wm[0]
    down_w = wm[1]
    hidden = bdot(left[0], up_w) + bias[...]
    phi = 0.5 * (1.0 + lax.erf(hidden * INV_ROOT_TWO))
    right[1] = (hidden * phi).astype(BF16)
    grad_act = bdot(left[1], down_w)
    slope = phi + hidden * jnp.exp(-0.5 * hidden * hidden) * INV_ROOT_TAU
    right[0] = (grad_act * slope).astype(BF16)

    s_g = sem_ids(1)
    gs[...] = bdot(left[1 - c], right[1 - c], TN_DIMS).reshape(NY, NX, RB, HID).astype(BF16)
    send(gs, grv, s_g, (sib, o))

    def scatter_z(value, buf, slots, s0):
        buf[...] = value.reshape(NZ, OWN_TOK, D).astype(BF16)
        for k in range(1, NZ):
            dest = lax.rem(o + k, NZ)
            send(buf.at[dest], slots.at[k - 1], s0 + k - 1, (t, dest))

    def scatter_z_sum(buf, slots, s0):
        total = buf[o].astype(F32)
        for k in range(1, NZ):
            arrived(slots.at[k - 1], s0 + k - 1)
            total = total + slots[k - 1].astype(F32)
        return total

    s_z = sem_ids(NZ - 1)
    s_b = sem_ids(NZ - 1)
    scatter_z(bdot(right[0], up_w, NT_DIMS), zs, zr, s_z)
    gf[...] = bdot(left[c], right[c], TN_DIMS).reshape(NY, NX, RB, HID)

    arrived(grv, s_g)
    pair = gf[...] + grv[...].astype(F32)
    gf[...] = pair
    gb[...] = pair.astype(BF16)
    s_rx = sem_ids(NX - 1)
    for k in range(1, NX):
        col = lax.rem(x + k, NX)
        send(gb.at[:, col], rx.at[k - 1], s_rx + k - 1, (tile_at(y, col), o))
    scatter_z(bdot(right[1], down_w, NT_DIMS), bs, br, s_b)

    for k in range(1, NX):
        arrived(rx.at[k - 1], s_rx + k - 1)
    xsum = gf[:, x] + rx[0].astype(F32) + rx[1].astype(F32) + rx[2].astype(F32)
    gx[...] = xsum
    ty[...] = xsum.astype(BF16)
    s_ry = sem_ids(NY - 1)
    for k in range(1, NY):
        row = lax.rem(y + k, NY)
        send(ty.at[row], ry.at[k - 1], s_ry + k - 1, (tile_at(row, x), o))

    grad_normed = scatter_z_sum(zs, zr, s_z)
    own_rows = pl.ds(pl.multiple_of(o * OWN_TOK, OWN_TOK), OWN_TOK)
    own_live = length > o // 2
    centred = mixed[own_rows, :]
    g = grad_normed * gain[...]
    mean1 = jnp.sum(g, axis=-1, keepdims=True) * (1.0 / D)
    mean2 = jnp.sum(g * centred, axis=-1, keepdims=True) * (1.0 / D)
    grad_mixed = inv_s[own_rows, :] * (g - mean1 - centred * mean2)
    grad_mixed = jnp.where(own_live, grad_mixed, 0.0)
    hg[...] = grad_mixed.astype(BF16)
    s_h = sem_ids(2)
    s_ct = sem_ids(4)
    s_ch = sem_ids(1)
    send(hg, nb.at[0], s_h, (t, lax.rem(o + 1, NZ)))
    send(hg, nb.at[1], s_h + 1, (t, lax.rem(o + NZ - 1, NZ)))
    s_c4 = sem_ids(4)

    @pl.when(first_own)
    def _():
        for q in range(4):
            pltpu.make_async_remote_copy(
                src_ref=hg, dst_ref=chd, send_sem=ss.at[s_c4 + q], recv_sem=rs.at[s_ch],
                device_id=(dn_t, 2 * q + 1), device_id_type=MESH,
            ).start()

    @pl.when(odd_own)
    def _():
        q = o // 2
        pltpu.make_async_remote_copy(
            src_ref=hg, dst_ref=ct.at[q], send_sem=ss.at[s_c4], recv_sem=rs.at[s_ct + q],
            device_id=(up_t, 0), device_id_type=MESH,
        ).start()

    frame2[...] = jnp.zeros_like(frame2)
    for ch in range(CH):
        frame2[ch, 3:7, 3:11, :] = grad_mixed[:, 128 * ch : 128 * ch + 128].reshape(4, 8, 128)

    for k in range(1, NY):
        arrived(ry.at[k - 1], s_ry + k - 1)
    total = gx[y]
    for k in range(1, NY):
        total = total + ry[k - 1].astype(F32)
    grow[...] = total
    ga[y, x] = total.astype(BF16)
    s_gy = sem_ids(NY - 1)
    s_gx = sem_ids(NX - 1)
    gather_y(ga, s_gy)

    def put_before(block):
        rows3 = block.astype(F32)[8:32]
        for ch in range(CH):
            frame2[ch, 0:3, 3:11, :] = rows3[:, 128 * ch : 128 * ch + 128].reshape(3, 8, 128)

    def put_after(block):
        rows3 = block.astype(F32)[0:24]
        for ch in range(CH):
            frame2[ch, 7:10, 3:11, :] = rows3[:, 128 * ch : 128 * ch + 128].reshape(3, 8, 128)

    arrived(nb.at[0], s_h)
    arrived(nb.at[1], s_h + 1)

    @pl.when(first_own)
    def _():
        for q in range(4):
            arrived(ct.at[q], s_ct + q)
        prev_len = lens[dn_t]
        block = ct[0].astype(F32)
        for q in range(1, 4):
            block = jnp.where(prev_len == q + 1, ct[q].astype(F32), block)
        put_before(jnp.where(t > 0, block, 0.0))
        for q in range(4):
            pltpu.make_async_remote_copy(
                src_ref=hg, dst_ref=chd, send_sem=ss.at[s_c4 + q], recv_sem=rs.at[s_ch],
                device_id=(dn_t, 2 * q + 1), device_id_type=MESH,
            ).wait_send()

    @pl.when(jnp.logical_not(first_own))
    def _():
        put_before(nb[0])

    @pl.when(odd_own)
    def _():
        arrived(chd, s_ch)
        q = o // 2
        edge = jnp.where(t < NT - 1, chd[...].astype(F32), 0.0)
        put_after(jnp.where(length == q + 1, edge, nb[1].astype(F32)))
        pltpu.make_async_remote_copy(
            src_ref=hg, dst_ref=ct.at[q], send_sem=ss.at[s_c4], recv_sem=rs.at[s_ct + q],
            device_id=(up_t, 0), device_id_type=MESH,
        ).wait_send()

    @pl.when(jnp.logical_not(odd_own))
    def _():
        put_after(nb[1])

    def chunk2(ch, _):
        lanes = pl.ds(pl.multiple_of(ch * 128, 128), 128)
        acc = jnp.zeros((4, 8, 128), F32)
        for i in range(7):
            for j in range(7):
                w = dk[6 - i, 6 - j : 7 - j, lanes].reshape(1, 1, 128)
                acc = acc + w * frame2[ch, i : i + 4, j : j + 8, :]
        res = cot[own_rows, lanes].astype(F32) + acc.reshape(OWN_TOK, 128)
        gout_ref[:, lanes] = jnp.where(own_live, res, 0.0).astype(BF16)
        return 0

    lax.fori_loop(0, CH, chunk2, 0)

    gather_y_wait(ga, s_gy)
    gather_x(ga, s_gx)

    branch = scatter_z_sum(bs, br, s_b)
    own_keep = jnp.where(own_live, tissue[o // 2, 0], 0).astype(F32)
    res = feat[own_rows, :].astype(F32) + (own_keep * scale[...]) * branch
    out_ref[...] = jnp.where(own_live, res, 0.0).astype(BF16)

    for k in range(1, NX):
        arrived(ga.at[:, lax.rem(x + NX - k, NX)], s_gx + k - 1)

    whole = ga[...].astype(F32).reshape(D, HID)
    norm2 = jnp.sum(jnp.sum(whole * whole, axis=0, keepdims=True), axis=1, keepdims=True)
    root = lax.rsqrt(norm2 + EPS_NORM)
    gm16[...] = whole.astype(BF16)
    g16 = gm16[...]
    gram = bdot(g16, g16, TN_DIMS) * (root * root)
    eye = (
        lax.broadcasted_iota(jnp.int32, (HID, HID), 0) == lax.broadcasted_iota(jnp.int32, (HID, HID), 1)
    ).astype(F32)

    def poly(a):
        return NS_A * eye + NS_B * a + NS_C * f32dot(a, a)

    p0 = poly(gram)
    gram1 = f32dot(f32dot(gram, p0), p0)
    p1 = poly(gram1)
    xo[c] = f32dot(f32dot(grow[...] * root, p0), p1)
    s_x = sem_ids(1)
    send(xo.at[c], xo.at[c], s_x, (sib, o))
    arrived(xo.at[1 - c], s_x)
    mu_ref[...] = jnp.where(c == 0, xo[0, 0:12, :], xo[0, 12:24, :])
    md_ref[...] = jnp.where(c == 0, xo[1, 0:12, :], xo[1, 12:24, :])

    for cp in sent:
        cp.wait_send()


SEMS = 96


def shards(features, cotangent, depth_kernel, ln_gain, weight_up, bias_up, weight_down, layer_scale, tissue, lengths):
    vmem = pl.BlockSpec(memory_space=pltpu.VMEM)
    smem = pl.BlockSpec(memory_space=pltpu.SMEM)
    block4 = (NY, NX, RB, HID)
    scratch = [
        pltpu.VMEM((2, 12, HID), BF16),
        pltpu.VMEM((12, HID), BF16),
        pltpu.VMEM((24, HID), F32),
        pltpu.VMEM((2,) + block4, BF16),
        pltpu.VMEM((2, D, HID), BF16),
        pltpu.VMEM((8, 128), F32),
        pltpu.VMEM((2, 24, D), BF16),
        pltpu.VMEM((2, 24, D), BF16),
        pltpu.VMEM((CH, 38, 16, 128), F32),
        pltpu.VMEM((TOK, D), F32),
        pltpu.VMEM((TOK, 1), F32),
        pltpu.VMEM((2, TOK, D), BF16),
        pltpu.VMEM((2, TOK, HID), BF16),
        pltpu.VMEM((NZ, OWN_TOK, D), BF16),
        pltpu.VMEM((NZ - 1, OWN_TOK, D), BF16),
        pltpu.VMEM((NZ, OWN_TOK, D), BF16),
        pltpu.VMEM((NZ - 1, OWN_TOK, D), BF16),
        pltpu.VMEM(block4, BF16),
        pltpu.VMEM(block4, BF16),
        pltpu.VMEM(block4, F32),
        pltpu.VMEM(block4, BF16),
        pltpu.VMEM((NX - 1, NY, RB, HID), BF16),
        pltpu.VMEM((NY, RB, HID), F32),
        pltpu.VMEM((NY, RB, HID), BF16),
        pltpu.VMEM((NY - 1, RB, HID), BF16),
        pltpu.VMEM((RB, HID), F32),
        pltpu.VMEM(block4, BF16),
        pltpu.VMEM((D, HID), BF16),
        pltpu.VMEM((OWN_TOK, D), BF16),
        pltpu.VMEM((2, OWN_TOK, D), BF16),
        pltpu.VMEM((4, OWN_TOK, D), BF16),
        pltpu.VMEM((OWN_TOK, D), BF16),
        pltpu.VMEM((CH, 10, 16, 128), F32),
        pltpu.VMEM((2, RB, HID), F32),
        pltpu.SemaphoreType.DMA((SEMS,)),
        pltpu.SemaphoreType.DMA((SEMS,)),
    ]
    outs = pl.pallas_call(
        body,
        out_shape=(
            jax.ShapeDtypeStruct((OWN_TOK, D), BF16),
            jax.ShapeDtypeStruct((OWN_TOK, D), BF16),
            jax.ShapeDtypeStruct((12, HID), F32),
            jax.ShapeDtypeStruct((12, HID), F32),
        ),
        in_specs=[smem, smem] + [vmem] * 8,
        out_specs=(vmem,) * 4,
        scratch_shapes=scratch,
        compiler_params=pltpu.CompilerParams(
            collective_id=0, has_side_effects=True, vmem_limit_bytes=48 << 20
        ),
    )(
        lengths,
        tissue,
        features.reshape(TOK, D),
        cotangent.reshape(TOK, D),
        depth_kernel,
        ln_gain.reshape(1, D),
        weight_up,
        bias_up.reshape(1, HID),
        weight_down.T,
        layer_scale.reshape(1, D),
    )
    block_out, grad_features, muon_up, muon_down_t = outs
    return (
        block_out.reshape(4, 8, D),
        grad_features.reshape(4, 8, D),
        muon_up,
        muon_down_t.T,
    )


def solution(mesh):
    in_specs = (
        P("tile", None, None),
        P("tile", None, None),
        P(),
        P(),
        P("tile", "own"),
        P("own"),
        P("own", "tile"),
        P(),
        P("tile", None),
        P(),
    )
    out_specs = (
        P(("tile", "own"), None, None),
        P(("tile", "own"), None, None),
        P("tile", "own"),
        P("own", "tile"),
    )
    return jax.shard_map(shards, mesh=mesh, in_specs=in_specs, out_specs=out_specs, check_vma=False)
```

time: 474 us -> 83.1 us (0.18); the launches traced: 467 us -> 82.8 us
  waiting for transfers between devices: 260 us -> 0 us
  blocking collectives: 97.7 us -> 0 us
  Pallas kernels: 0 us -> 73.9 us
  matrix products: 37.6 us -> 0 us
  other arithmetic: 23.7 us -> 0 us
  starting transfers between devices: 21 us -> 0 us
  between operations: 19.3 us -> 0.67 us
    psum x2 -> x0, waiting for transfers between devices: 240 us -> none  [the longest x1 168 us: shards(): whole_up, whole_down = lax.psum((grad_up, grad_down), 'tile')]
    all_gather x2 -> x0, blocking collectives: 97.7 us -> none  [the longest x1 49.7 us: shards(): down_full = lax.all_gather(weight_down, 'tile', axis=1, tiled=True)]
    pallas_call x0 -> x1, Pallas kernels: none -> 73.9 us  [shards(): pl.pallas_call(body, out_shape=(jax.ShapeDtypeStruct((OWN_TOK, D), BF16),...]
    dot_general x18 -> x0, matrix products: 37.6 us -> none  [the longest x4 18.1 us: ns_update(): jnp.dot(block, polynomial, precision=HIGHEST_PREC, preferred_element_type...]
    ppermute x4 -> x0, starting transfers between devices: 20.7 us -> none  [the longest x2 10.7 us: padded_2(): after = lax.ppermute(initial, axis, down)]
    reduce_scatter x1 -> x0, waiting for transfers between devices: 18 us -> none  [shards(): lax.psum_scatter(branch.reshape(tile_rows, columns, channels).astype(jnp....]
    reduce_sum x5 -> x0, other arithmetic: 11.3 us -> none  [the longest x1 6.97 us: layer_norm(): average = jnp.mean(mixed, axis=-1, keepdims=True)]
    add x2 -> x0, other arithmetic: 6.69 us -> none  [the longest x1 6.08 us: depthwise(): totals + kernel[row_tap, col_tap] * padded[row_tap:row_tap + row_count, c...]
  transfers between devices with their start and end apart: 7 -> 0, of which waited for: 4 -> 0; matrix products, arithmetic and copies ran while one was open for 5% -> 0% of each run, Pallas kernels for 0% -> 0%
where the time goes in v1:
time: 83.1 us; the launch traced here: 82.8 us
  Pallas kernels  73.9 us (89%)
  local copies, waits for them, and re-layouts  8.2 us (10%)
    pallas_call x1, Pallas kernels, shards(): pl.pallas_call(body, out_shape=(jax.ShapeDtypeStruct((OWN_TOK, D), BF16),...  73.9 us
    unnamed x17, local copies, waits for them, and re-layouts  6.11 us

profile of v1, /device:TPU:1, one launch (start us, length us, event | category | flops | bytes accessed | tf_op | source)
XLA Modules:
  0.0 82.8 jit_solution(11831059587183527693)
XLA Ops:
  0.6 0.0 copy-start.4
  0.6 0.0 copy-start.3
  0.7 0.7 reshape.32.bias
  1.3 0.7 copy.14.tissue
  2.1 0.7 reshape.31.gain
  2.8 0.0 copy-start.5
  2.8 0.7 reshape.33.scale
  3.5 0.0 copy-done.4
  3.5 0.0 copy-done.3
  3.5 0.0 copy-done.5
  3.5 0.0 copy-start
  3.5 1.0 %copy-done = bf16[32,8,768]{2,1,0:T(8,128)(2,1)S(1)} copy-done((bf16[32,8,768]{2,1,0:T(8,128)(2,1)S(1)}, bf16[32,8,768]{2,1,0:T(8,128)(2,1)}, u32[]{:S(2)}) %copy-start) | copy-done | bytes 393240
  4.5 0.0 copy-start.1
  4.5 1.0 %copy-done.1 = bf16[32,8,768]{2,1,0:T(8,128)(2,1)S(1)} copy-done((bf16[32,8,768]{2,1,0:T(8,128)(2,1)S(1)}, bf16[32,8,768]{2,1,0:T(8,128)(2,1)}, u32[]{:S(2)}) %copy-start.1) | copy-done | bytes 393240
  5.5 0.0 copy-start.2
  5.5 0.9 %copy-done.2 = f32[7,7,768]{2,1,0:T(8,128)S(1)} copy-done((f32[7,7,768]{2,1,0:T(8,128)S(1)}, f32[7,7,768]{2,1,0:T(8,128)}, u32[]{:S(2)}) %copy-start.2) | copy-done | bytes 150552
  6.4 73.9 %shard_map.129 = (bf16[32,768]{1,0:T(8,128)(2,1)S(1)}, bf16[32,768]{1,0:T(8,128)(2,1)S(1)}, f32[12,384]{1,0:T(8,128)S(1)}, f32[12,384]{1,0:T(8,128)S(1)}) custom-call(s32[64]{0:T(128)S(1)} %copy-done.5, s32[4,1]{1,0:T(4,128)S(1)} %copy.14.tissue, bf16[256,768]{1,0:T(8,128)(2,1)S(1)} %bitcast.6, bf16[256,768]{1,0:T(8,128)(2,1)S(1)} %bitcast.7, ...), custom_call_target="tpu_custom_call" | custom-call | tf_op jit(solution)/shard_map/pallas_call | solution.py:461
  80.3 0.6 copy.19
  81.0 0.6 copy.20
  81.6 0.6 copy.21
  82.2 0.6 copy.22
Async XLA Ops:
  0.6 2.9 %copy-start.4 = (bf16[384,12]{0,1:T(8,128)(2,1)S(1)}, bf16[384,12]{0,1:T(8,128)(2,1)}, u32[]{:S(2)}) copy-start(bf16[384,12]{0,1:T(8,128)(2,1)} %param.16) | copy-start | bytes 27652
  0.6 2.8 %copy-start.3 = (bf16[12,384]{1,0:T(8,128)(2,1)S(1)}, bf16[12,384]{1,0:T(8,128)(2,1)}, u32[]{:S(2)}) copy-start(bf16[12,384]{1,0:T(8,128)(2,1)} %wu.1) | copy-start | bytes 27652
  2.8 0.7 copy-start.5
  3.5 1.0 %copy-start = (bf16[32,8,768]{2,1,0:T(8,128)(2,1)S(1)}, bf16[32,8,768]{2,1,0:T(8,128)(2,1)}, u32[]{:S(2)}) copy-start(bf16[32,8,768]{2,1,0:T(8,128)(2,1)} %param.10) | copy-start | bytes 1179652
  4.5 1.0 %copy-start.1 = (bf16[32,8,768]{2,1,0:T(8,128)(2,1)S(1)}, bf16[32,8,768]{2,1,0:T(8,128)(2,1)}, u32[]{:S(2)}) copy-start(bf16[32,8,768]{2,1,0:T(8,128)(2,1)} %param.11) | copy-start | bytes 1179652
  5.5 0.9 %copy-start.2 = (f32[7,7,768]{2,1,0:T(8,128)S(1)}, f32[7,7,768]{2,1,0:T(8,128)}, u32[]{:S(2)}) copy-start(f32[7,7,768]{2,1,0:T(8,128)} %dk.1) | copy-start | bytes 451588

commit v2 on v1

--- a/solution.py
+++ b/solution.py
@@ -40,11 +40,11 @@
 
 
 def body(
-    lens, tissue, feat, cot, dk, gain, wu, bias, wd, scale,
+    lens_h, tissue_h, feat_h, cot_h, dk_h, gain_h, wu_h, bias_h, wd_h, scale_h,
     out_ref, gout_ref, mu_ref, md_ref,
-    pieces, piece_in, t24, wg, wm, fx, rim, halo, frame, mixed, inv_s, left, right,
-    zs, zr, bs, br, gs, grv, gf, gb, rx, gx, ty, ry, grow, ga, gm16, hg, nb, ct, chd, frame2, xo,
-    ss, rs,
+    lens, tissue, feat, cot, dk, gain1, bias1, scale1, pieces, piece_in, t24, wg, wm, rim, halo, frame, mixed, inv_s, left, right,
+    zs, zr, bs, br, gs, grv, gf, gb, rx, ty, ry, grow, ga, gm16, hg, nb, ct, chd, frame2, xo,
+    ss, rs, ls,
 ):
     t = lax.axis_index("tile")
     o = lax.axis_index("own")
@@ -78,6 +78,17 @@
 
     def arrived(dst, sem):
         copy(dst, dst, sem, (t, o)).wait_recv()
+
+    fetches = {}
+    for n, (name, src, dst) in enumerate(
+        (
+            ("wu", wu_h, pieces.at[0]), ("wd", wd_h, pieces.at[1]), ("lens", lens_h, lens),
+            ("feat", feat_h, feat), ("tissue", tissue_h, tissue), ("dk", dk_h, dk), ("gain", gain_h, gain1),
+            ("scale", scale_h, scale1), ("cot", cot_h, cot), ("bias", bias_h, bias1),
+        )
+    ):
+        fetches[name] = pltpu.make_async_copy(src, dst, ls.at[n])
+        fetches[name].start()
 
     bar = pltpu.get_barrier_semaphore()
 
@@ -107,36 +118,25 @@
     def _():
         greet((up_t, 0))
 
+    expected = 1 + (NY - 1) + (NX - 1) + (NZ - 1) + 2
+    fetches["wu"].wait()
+    fetches["wd"].wait()
+    pl.semaphore_wait(bar, expected + 4 * ((NZ - o) // NZ) + lax.rem(o, 2))
+
+    s_piece = sem_ids(1)
+    send(pieces.at[1 - c], piece_in, s_piece, (sib, o))
+
+    fetches["lens"].wait()
+    fetches["feat"].wait()
     length = lens[t]
-
-    pieces[0] = wu[...]
-    pieces[1] = wd[...]
     rim[0] = feat[0:24, :].astype(F32).astype(BF16)
     tail = feat[0:64, :].astype(F32)[40:64]
     for q in range(1, 4):
         tail = jnp.where(length == q + 1, feat[64 * q : 64 * q + 64, :].astype(F32)[40:64], tail)
     rim[1] = tail.astype(BF16)
-
-    expected = 1 + (NY - 1) + (NX - 1) + (NZ - 1) + 2
-    pl.semaphore_wait(bar, expected + 4 * ((NZ - o) // NZ) + lax.rem(o, 2))
-
-    s_piece = sem_ids(1)
-    send(pieces.at[1 - c], piece_in, s_piece, (sib, o))
     s_halo = sem_ids(2)
     send(rim.at[1], halo.at[0], s_halo, (up_t, o))
     send(rim.at[0], halo.at[1], s_halo + 1, (dn_t, o))
-
-    frame[...] = jnp.zeros_like(frame)
-    for q in range(4):
-        rows = slice(64 * q, 64 * q + 64)
-        live = length > q
-        keep = jnp.where(live, tissue[q, 0], 0).astype(F32)
-        f = feat[rows, :].astype(F32)
-        if q:
-            f = jnp.where(live, f, 0.0)
-        for ch in range(CH):
-            frame[ch, 3 + 8 * q : 11 + 8 * q, 3:11, :] = f[:, 128 * ch : 128 * ch + 128].reshape(8, 8, 128)
-        left[1, rows, :] = ((keep * scale[...]) * cot[rows, :].astype(F32)).astype(BF16)
 
     arrived(piece_in, s_piece)
     mine = pieces[c].astype(F32)
@@ -145,23 +145,55 @@
     t24[12:24, :] = jnp.where(c == 0, other, mine)
     wg[c, y, x] = t24[...].astype(BF16)
 
-    def gather_y(buf, s0):
-        for k in range(1, NY):
-            send(buf.at[y, x], buf.at[y, x], s0 + k - 1, (tile_at(lax.rem(y + k, NY), x), o))
-
-    def gather_y_wait(buf, s0):
-        for k in range(1, NY):
-            arrived(buf.at[lax.rem(y + NY - k, NY), x], s0 + k - 1)
-
-    def gather_x(buf, s0):
+    near = (1, 7, 2, 6, 3, 5, 4)
+    far = near[::-1]
+
+    def row_of(k):
+        return lax.rem(y + NY - k, NY)
+
+    def share_x(buf, row, sem):
         for k in range(1, NX):
-            send(buf.at[:, x], buf.at[:, x], s0 + k - 1, (tile_at(y, lax.rem(x + k, NX)), o))
+            send(buf.at[row, x], buf.at[row, x], sem + k - 1, (tile_at(y, lax.rem(x + k, NX)), o))
+
+    def gather_start(buf, s_y, s_x):
+        for k in far:
+            send(buf.at[y, x], buf.at[y, x], s_y + k - 1, (tile_at(lax.rem(y + k, NY), x), o))
+        share_x(buf, y, s_x)
+
+    def gather_relay(buf, s_y, s_x, ks):
+        for k in ks:
+            row = row_of(k)
+            arrived(buf.at[row, x], s_y + k - 1)
+            share_x(buf, row, s_x + 3 * k)
+
+    def gather_row(buf, s_x, k):
+        row = row_of(k)
+        for n in range(1, NX):
+            arrived(buf.at[row, lax.rem(x + NX - n, NX)], s_x + 3 * k + n - 1)
+        return row
 
     s_wy = sem_ids(NY - 1)
-    s_wx = sem_ids(NX - 1)
-    s_ws = sem_ids(NX)
+    s_wx = sem_ids(3 * NY)
+    s_ws = sem_ids(NY)
     wg_c = wg.at[c]
-    gather_y(wg_c, s_wy)
+    wg_o = wg.at[1 - c]
+    gather_start(wg_c, s_wy, s_wx)
+
+    for name in ("tissue", "dk", "gain", "scale", "cot", "bias"):
+        fetches[name].wait()
+    gain = gain1[...].reshape(1, D)
+    scale = scale1[...].reshape(1, D)
+    frame[...] = jnp.zeros_like(frame)
+    for q in range(4):
+        rows = slice(64 * q, 64 * q + 64)
+        live = length > q
+        keep = jnp.where(live, tissue[q], 0).astype(F32)
+        f = feat[rows, :].astype(F32)
+        if q:
+            f = jnp.where(live, f, 0.0)
+        for ch in range(CH):
+            frame[ch, 3 + 8 * q : 11 + 8 * q, 3:11, :] = f[:, 128 * ch : 128 * ch + 128].reshape(8, 8, 128)
+        left[1, rows, :] = ((keep * scale) * cot[rows, :].astype(F32)).astype(BF16)
 
     arrived(halo.at[0], s_halo)
     arrived(halo.at[1], s_halo + 1)
@@ -190,10 +222,9 @@
         lax.fori_loop(0, CH, chunk, 0)
 
     conv_half(0)
-    gather_y_wait(wg_c, s_wy)
-    gather_x(wg_c, s_wx)
-    send(wg_c.at[:, x], wg_c.at[:, x], s_ws, (sib, o))
+    gather_relay(wg_c, s_wy, s_wx, near[:4])
     conv_half(1)
+    gather_relay(wg_c, s_wy, s_wx, near[4:6])
 
     for q in range(4):
         rows = slice(64 * q, 64 * q + 64)
@@ -204,21 +235,25 @@
         centred = shifted * inv
         mixed[rows, :] = centred
         inv_s[rows, :] = inv
-        left[0, rows, :] = (centred * gain[...]).astype(BF16)
-
-    for k in range(1, NX):
-        col = lax.rem(x + NX - k, NX)
-        arrived(wg_c.at[:, col], s_wx + k - 1)
-        send(wg_c.at[:, col], wg_c.at[:, col], s_ws + k, (sib, o))
-    wm[c] = wg[c].astype(F32).reshape(D, HID).astype(BF16)
-    wg_o = wg.at[1 - c]
-    for k in range(NX):
-        arrived(wg_o.at[:, lax.rem(x + NX - k, NX)], s_ws + k)
-    wm[1 - c] = wg[1 - c].astype(F32).reshape(D, HID).astype(BF16)
-
-    up_w = wm[0]
-    down_w = wm[1]
-    hidden = bdot(left[0], up_w) + bias[...]
+        left[0, rows, :] = (centred * gain).astype(BF16)
+
+    gather_relay(wg_c, s_wy, s_wx, near[6:])
+
+    def take(m, row):
+        wm[m, row] = wg[m, row].astype(F32).reshape(96, HID).astype(BF16)
+
+    for k in (0,) + near:
+        row = gather_row(wg_c, s_wx, k)
+        send(wg_c.at[row], wg_c.at[row], s_ws + k, (sib, o))
+        take(c, row)
+    for k in (0,) + near:
+        row = row_of(k)
+        arrived(wg_o.at[row], s_ws + k)
+        take(1 - c, row)
+
+    up_w = wm[0].reshape(D, HID)
+    down_w = wm[1].reshape(D, HID)
+    hidden = bdot(left[0], up_w) + bias1[...].reshape(1, HID)
     phi = 0.5 * (1.0 + lax.erf(hidden * INV_ROOT_TWO))
     right[1] = (hidden * phi).astype(BF16)
     grad_act = bdot(left[1], down_w)
@@ -231,7 +266,7 @@
 
     def scatter_z(value, buf, slots, s0):
         buf[...] = value.reshape(NZ, OWN_TOK, D).astype(BF16)
-        for k in range(1, NZ):
+        for k in far:
             dest = lax.rem(o + k, NZ)
             send(buf.at[dest], slots.at[k - 1], s0 + k - 1, (t, dest))
 
@@ -244,34 +279,45 @@
 
     s_z = sem_ids(NZ - 1)
     s_b = sem_ids(NZ - 1)
+    gf[...] = bdot(left[c], right[c], TN_DIMS).reshape(NY, NX, RB, HID)
     scatter_z(bdot(right[0], up_w, NT_DIMS), zs, zr, s_z)
-    gf[...] = bdot(left[c], right[c], TN_DIMS).reshape(NY, NX, RB, HID)
-
+
+    s_rx = sem_ids(3 * NY)
+    s_ry = sem_ids(NY - 1)
     arrived(grv, s_g)
-    pair = gf[...] + grv[...].astype(F32)
-    gf[...] = pair
-    gb[...] = pair.astype(BF16)
-    s_rx = sem_ids(NX - 1)
-    for k in range(1, NX):
-        col = lax.rem(x + k, NX)
-        send(gb.at[:, col], rx.at[k - 1], s_rx + k - 1, (tile_at(y, col), o))
+    for k in far + (0,):
+        row = lax.rem(y + k, NY)
+        pair = gf[row] + grv[row].astype(F32)
+        gf[row] = pair
+        gb[row] = pair.astype(BF16)
+        for n in range(1, NX):
+            col = lax.rem(x + n, NX)
+            send(gb.at[row, col], rx.at[row, n - 1], s_rx + 3 * k + n - 1, (tile_at(y, col), o))
     scatter_z(bdot(right[1], down_w, NT_DIMS), bs, br, s_b)
-
-    for k in range(1, NX):
-        arrived(rx.at[k - 1], s_rx + k - 1)
-    xsum = gf[:, x] + rx[0].astype(F32) + rx[1].astype(F32) + rx[2].astype(F32)
-    gx[...] = xsum
-    ty[...] = xsum.astype(BF16)
-    s_ry = sem_ids(NY - 1)
-    for k in range(1, NY):
+    total = None
+    for k in far + (0,):
         row = lax.rem(y + k, NY)
-        send(ty.at[row], ry.at[k - 1], s_ry + k - 1, (tile_at(row, x), o))
+        total = gf[row, x]
+        for n in range(1, NX):
+            arrived(rx.at[row, n - 1], s_rx + 3 * k + n - 1)
+            total = total + rx[row, n - 1].astype(F32)
+        if k:
+            ty[row] = total.astype(BF16)
+            send(ty.at[row], ry.at[k - 1], s_ry + k - 1, (tile_at(row, x), o))
+    for k in near:
+        arrived(ry.at[k - 1], s_ry + k - 1)
+        total = total + ry[k - 1].astype(F32)
+    grow[...] = total
+    ga[y, x] = total.astype(BF16)
+    s_gy = sem_ids(NY - 1)
+    s_gx = sem_ids(3 * NY)
+    gather_start(ga, s_gy, s_gx)
 
     grad_normed = scatter_z_sum(zs, zr, s_z)
     own_rows = pl.ds(pl.multiple_of(o * OWN_TOK, OWN_TOK), OWN_TOK)
     own_live = length > o // 2
     centred = mixed[own_rows, :]
-    g = grad_normed * gain[...]
+    g = grad_normed * gain
     mean1 = jnp.sum(g, axis=-1, keepdims=True) * (1.0 / D)
     mean2 = jnp.sum(g * centred, axis=-1, keepdims=True) * (1.0 / D)
     grad_mixed = inv_s[own_rows, :] * (g - mean1 - centred * mean2)
@@ -304,16 +350,7 @@
     for ch in range(CH):
         frame2[ch, 3:7, 3:11, :] = grad_mixed[:, 128 * ch : 128 * ch + 128].reshape(4, 8, 128)
 
-    for k in range(1, NY):
-        arrived(ry.at[k - 1], s_ry + k - 1)
-    total = gx[y]
-    for k in range(1, NY):
-        total = total + ry[k - 1].astype(F32)
-    grow[...] = total
-    ga[y, x] = total.astype(BF16)
-    s_gy = sem_ids(NY - 1)
-    s_gx = sem_ids(NX - 1)
-    gather_y(ga, s_gy)
+    gather_relay(ga, s_gy, s_gx, near[:4])
 
     def put_before(block):
         rows3 = block.astype(F32)[8:32]
@@ -325,6 +362,7 @@
         for ch in range(CH):
             frame2[ch, 7:10, 3:11, :] = rows3[:, 128 * ch : 128 * ch + 128].reshape(3, 8, 128)
 
+    gather_relay(ga, s_gy, s_gx, near[4:])
     arrived(nb.at[0], s_h)
     arrived(nb.at[1], s_h + 1)
 
@@ -375,26 +413,26 @@
 
     lax.fori_loop(0, CH, chunk2, 0)
 
-    gather_y_wait(ga, s_gy)
-    gather_x(ga, s_gx)
-
     branch = scatter_z_sum(bs, br, s_b)
-    own_keep = jnp.where(own_live, tissue[o // 2, 0], 0).astype(F32)
-    res = feat[own_rows, :].astype(F32) + (own_keep * scale[...]) * branch
+    own_keep = jnp.where(own_live, tissue[o // 2], 0).astype(F32)
+    res = feat[own_rows, :].astype(F32) + (own_keep * scale) * branch
     out_ref[...] = jnp.where(own_live, res, 0.0).astype(BF16)
 
-    for k in range(1, NX):
-        arrived(ga.at[:, lax.rem(x + NX - k, NX)], s_gx + k - 1)
-
-    whole = ga[...].astype(F32).reshape(D, HID)
-    norm2 = jnp.sum(jnp.sum(whole * whole, axis=0, keepdims=True), axis=1, keepdims=True)
-    root = lax.rsqrt(norm2 + EPS_NORM)
-    gm16[...] = whole.astype(BF16)
-    g16 = gm16[...]
-    gram = bdot(g16, g16, TN_DIMS) * (root * root)
+    def gram_of(ks):
+        for n, k in enumerate(ks):
+            row = gather_row(ga, s_gx, k)
+            gm16[n] = ga[row].astype(F32).reshape(96, HID).astype(BF16)
+        g16 = gm16[0 : len(ks)].reshape(96 * len(ks), HID)
+        return bdot(g16, g16, TN_DIMS)
+
+    gram = gram_of((0,) + near[:4]) + gram_of(near[4:])
     eye = (
         lax.broadcasted_iota(jnp.int32, (HID, HID), 0) == lax.broadcasted_iota(jnp.int32, (HID, HID), 1)
     ).astype(F32)
+
+    norm2 = jnp.sum(jnp.sum(gram * eye, axis=0, keepdims=True), axis=1, keepdims=True)
+    root = lax.rsqrt(norm2 + EPS_NORM)
+    gram = gram * (root * root)
 
     def poly(a):
         return NS_A * eye + NS_B * a + NS_C * f32dot(a, a)
@@ -413,20 +451,27 @@
         cp.wait_send()
 
 
-SEMS = 96
+SEMS = 160
 
 
 def shards(features, cotangent, depth_kernel, ln_gain, weight_up, bias_up, weight_down, layer_scale, tissue, lengths):
     vmem = pl.BlockSpec(memory_space=pltpu.VMEM)
-    smem = pl.BlockSpec(memory_space=pltpu.SMEM)
+    hbm = pl.BlockSpec(memory_space=pltpu.HBM)
     block4 = (NY, NX, RB, HID)
     scratch = [
+        pltpu.SMEM((NT,), jnp.int32),
+        pltpu.SMEM((4,), jnp.int32),
+        pltpu.VMEM((TOK, D), BF16),
+        pltpu.VMEM((TOK, D), BF16),
+        pltpu.VMEM((7, 7, D), F32),
+        pltpu.VMEM((D,), F32),
+        pltpu.VMEM((HID,), F32),
+        pltpu.VMEM((D,), F32),
         pltpu.VMEM((2, 12, HID), BF16),
         pltpu.VMEM((12, HID), BF16),
         pltpu.VMEM((24, HID), F32),
         pltpu.VMEM((2,) + block4, BF16),
-        pltpu.VMEM((2, D, HID), BF16),
-        pltpu.VMEM((8, 128), F32),
+        pltpu.VMEM((2, NY, 96, HID), BF16),
         pltpu.VMEM((2, 24, D), BF16),
         pltpu.VMEM((2, 24, D), BF16),
         pltpu.VMEM((CH, 38, 16, 128), F32),
@@ -442,13 +487,12 @@
         pltpu.VMEM(block4, BF16),
         pltpu.VMEM(block4, F32),
         pltpu.VMEM(block4, BF16),
-        pltpu.VMEM((NX - 1, NY, RB, HID), BF16),
-        pltpu.VMEM((NY, RB, HID), F32),
+        pltpu.VMEM((NY, NX - 1, RB, HID), BF16),
         pltpu.VMEM((NY, RB, HID), BF16),
         pltpu.VMEM((NY - 1, RB, HID), BF16),
         pltpu.VMEM((RB, HID), F32),
         pltpu.VMEM(block4, BF16),
-        pltpu.VMEM((D, HID), BF16),
+        pltpu.VMEM((NY, 96, HID), BF16),
         pltpu.VMEM((OWN_TOK, D), BF16),
         pltpu.VMEM((2, OWN_TOK, D), BF16),
         pltpu.VMEM((4, OWN_TOK, D), BF16),
@@ -457,6 +501,7 @@
         pltpu.VMEM((2, RB, HID), F32),
         pltpu.SemaphoreType.DMA((SEMS,)),
         pltpu.SemaphoreType.DMA((SEMS,)),
+        pltpu.SemaphoreType.DMA((10,)),
     ]
     outs = pl.pallas_call(
         body,
@@ -466,7 +511,7 @@
             jax.ShapeDtypeStruct((12, HID), F32),
             jax.ShapeDtypeStruct((12, HID), F32),
         ),
-        in_specs=[smem, smem] + [vmem] * 8,
+        in_specs=[hbm] * 10,
         out_specs=(vmem,) * 4,
         scratch_shapes=scratch,
         compiler_params=pltpu.CompilerParams(
@@ -474,15 +519,15 @@
         ),
     )(
         lengths,
-        tissue,
+        tissue.reshape(4),
         features.reshape(TOK, D),
         cotangent.reshape(TOK, D),
         depth_kernel,
-        ln_gain.reshape(1, D),
+        ln_gain,
         weight_up,
-        bias_up.reshape(1, HID),
+        bias_up,
         weight_down.T,
-        layer_scale.reshape(1, D),
+        layer_scale,
     )
     block_out, grad_features, muon_up, muon_down_t = outs
     return (

time: 83.1 us -> 74.9 us (0.901)
  Pallas kernels: 73.9 us -> 65.7 us
    pallas_call x1, Pallas kernels: 73.9 us -> 65.7 us  [shards(): pl.pallas_call(body, out_shape=(jax.ShapeDtypeStruct((OWN_TOK, D), BF16),...]
    reshape x3 -> x0, local copies, waits for them, and re-layouts: 2.09 us -> none  [the longest x1 0.7 us: shards(): layer_scale.reshape(1, D)]
    unnamed x17 -> x24, local copies, waits for them, and re-layouts: 6.11 us -> 8.14 us
where the time goes in v2:
time: 74.9 us; the launch traced here: 74.6 us
  Pallas kernels  65.7 us (88%)
  local copies, waits for them, and re-layouts  8.14 us (11%)
    pallas_call x1, Pallas kernels, shards(): pl.pallas_call(body, out_shape=(jax.ShapeDtypeStruct((OWN_TOK, D), BF16),...  65.7 us
    unnamed x24, local copies, waits for them, and re-layouts  8.14 us

profile of v2, /device:TPU:1, one launch (start us, length us, event | category | flops | bytes accessed | tf_op | source)
XLA Modules:
  0.0 74.6 jit_solution(16629231397601502622)
XLA Ops:
  0.6 0.0 copy-start.5
  0.6 0.0 copy-start.7
  0.7 0.0 copy-start.8
  0.7 0.0 copy-start.9
  0.7 0.6 copy-done.5
  1.3 0.0 copy-done.7
  1.3 0.0 copy-done.8
  1.3 0.0 copy-done.9
  1.3 0.0 copy-start
  1.3 1.0 %copy-done = bf16[32,8,768]{2,1,0:T(8,128)(2,1)S(1)} copy-done((bf16[32,8,768]{2,1,0:T(8,128)(2,1)S(1)}, bf16[32,8,768]{2,1,0:T(8,128)(2,1)}, u32[]{:S(2)}) %copy-start) | copy-done | bytes 393240
  2.3 0.0 copy-start.1
  2.3 1.0 %copy-done.1 = bf16[32,8,768]{2,1,0:T(8,128)(2,1)S(1)} copy-done((bf16[32,8,768]{2,1,0:T(8,128)(2,1)S(1)}, bf16[32,8,768]{2,1,0:T(8,128)(2,1)}, u32[]{:S(2)}) %copy-start.1) | copy-done | bytes 393240
  3.3 0.0 copy-start.2
  3.3 0.9 %copy-done.2 = f32[7,7,768]{2,1,0:T(8,128)S(1)} copy-done((f32[7,7,768]{2,1,0:T(8,128)S(1)}, f32[7,7,768]{2,1,0:T(8,128)}, u32[]{:S(2)}) %copy-start.2) | copy-done | bytes 150552
  4.3 0.0 copy-start.3
  4.3 0.7 copy-done.3
  5.0 0.0 copy-start.4
  5.0 0.7 copy-done.4
  5.7 0.0 copy-start.6
  5.7 0.7 copy-done.6
  6.4 65.7 %shard_map.129 = (bf16[32,768]{1,0:T(8,128)(2,1)S(1)}, bf16[32,768]{1,0:T(8,128)(2,1)S(1)}, f32[12,384]{1,0:T(8,128)S(1)}, f32[12,384]{1,0:T(8,128)S(1)}) custom-call(s32[64]{0:T(128)S(1)} %copy-done.8, s32[4]{0:T(128)S(1)} %bitcast.13, bf16[256,768]{1,0:T(8,128)(2,1)S(1)} %bitcast.7, bf16[256,768]{1,0:T(8,128)(2,1)S(1)} %bitcast.8, ...), custom_call_target="tpu_custom_call" | custom-call | tf_op jit(solution)/shard_map/pallas_call | solution.py:506
  72.1 0.6 copy.18
  72.7 0.6 copy.19
  73.3 0.6 copy.20
  73.9 0.6 copy.21
Async XLA Ops:
  0.6 0.7 copy-start.5
  0.6 0.7 copy-start.7
  0.7 0.7 copy-start.8
  0.7 0.7 copy-start.9
  1.3 1.0 %copy-start = (bf16[32,8,768]{2,1,0:T(8,128)(2,1)S(1)}, bf16[32,8,768]{2,1,0:T(8,128)(2,1)}, u32[]{:S(2)}) copy-start(bf16[32,8,768]{2,1,0:T(8,128)(2,1)} %param.10) | copy-start | bytes 1179652
  2.3 1.0 %copy-start.1 = (bf16[32,8,768]{2,1,0:T(8,128)(2,1)S(1)}, bf16[32,8,768]{2,1,0:T(8,128)(2,1)}, u32[]{:S(2)}) copy-start(bf16[32,8,768]{2,1,0:T(8,128)(2,1)} %param.11) | copy-start | bytes 1179652
  3.3 0.9 %copy-start.2 = (f32[7,7,768]{2,1,0:T(8,128)S(1)}, f32[7,7,768]{2,1,0:T(8,128)}, u32[]{:S(2)}) copy-start(f32[7,7,768]{2,1,0:T(8,128)} %dk_h.1) | copy-start | bytes 451588
  4.3 0.7 copy-start.3
  5.0 0.7 copy-start.4
  5.7 0.7 copy-start.6

commit v3 on v2

--- a/solution.py
+++ b/solution.py
@@ -515,7 +515,7 @@
         out_specs=(vmem,) * 4,
         scratch_shapes=scratch,
         compiler_params=pltpu.CompilerParams(
-            collective_id=0, has_side_effects=True, vmem_limit_bytes=48 << 20
+            collective_id=0, has_side_effects=True, vmem_limit_bytes=62 << 20
         ),
     )(
         lengths,

time: 74.9 us -> 70.3 us (0.939)
  local copies, waits for them, and re-layouts: 8.14 us -> 3.53 us
    unnamed x24 -> x10, local copies, waits for them, and re-layouts: 8.14 us -> 3.53 us
where the time goes in v3:
time: 70.3 us; the launch traced here: 69.9 us
  Pallas kernels  65.8 us (94%)
  local copies, waits for them, and re-layouts  3.53 us (5%)
    pallas_call x1, Pallas kernels, shards(): pl.pallas_call(body, out_shape=(jax.ShapeDtypeStruct((OWN_TOK, D), BF16),...  65.8 us
    unnamed x10, local copies, waits for them, and re-layouts  3.53 us

profile of v3, /device:TPU:1, one launch (start us, length us, event | category | flops | bytes accessed | tf_op | source)
XLA Modules:
  0.0 69.9 jit_solution(11924648372801694191)
XLA Ops:
  0.6 65.8 %shard_map.129 = (bf16[32,768]{1,0:T(8,128)(2,1)}, bf16[32,768]{1,0:T(8,128)(2,1)}, f32[12,384]{1,0:T(8,128)}, f32[12,384]{1,0:T(8,128)}) custom-call(s32[64]{0:T(128)} %lens_h.1, s32[4]{0:T(128)} %bitcast.13, bf16[256,768]{1,0:T(8,128)(2,1)} %bitcast.7, bf16[256,768]{1,0:T(8,128)(2,1)} %bitcast.8, f32[7,7,768]{2,1,0:T(8,128)} %dk_h.1, f32[768]{0:T(1024)} %gain_h.1, ...), custom_call_target="tpu_custom_call" | custom-call | tf_op jit(solution)/shard_map/pallas_call | solution.py:506
  66.4 0.0 copy-start
  66.4 1.4 %copy.18 = bf16[4,8,768]{2,1,0:T(8,128)(2,1)} copy(bf16[4,8,768]{2,1,0:T(8,128)(2,1)} %bitcast.10) | data formatting | bytes 98304
  67.8 0.0 copy-done
  67.8 0.0 copy-start.2
  67.9 0.6 copy.19
  68.5 0.1 copy-done.2
  68.6 0.0 copy-start.1
  68.6 0.6 copy.20
  69.2 0.1 copy-done.1
  69.3 0.6 copy.21
Async XLA Ops:
  66.4 1.4 %copy-start = (bf16[32,768]{1,0:T(8,128)(2,1)S(1)}, bf16[32,768]{1,0:T(8,128)(2,1)}, u32[]{:S(2)}) copy-start(bf16[32,768]{1,0:T(8,128)(2,1)} %get-tuple-element.9) | copy-start | bytes 147460
  67.8 0.7 %copy-start.2 = (f32[12,384]{1,0:T(8,128)S(1)}, f32[12,384]{1,0:T(8,128)}, u32[]{:S(2)}) copy-start(f32[12,384]{1,0:T(8,128)} %get-tuple-element.18) | copy-start | bytes 55300
  68.6 0.7 %copy-start.1 = (f32[12,384]{1,0:T(8,128)S(1)}, f32[12,384]{1,0:T(8,128)}, u32[]{:S(2)}) copy-start(f32[12,384]{1,0:T(8,128)} %get-tuple-element.11) | copy-start | bytes 55300

commit v4 on v3

--- a/solution.py
+++ b/solution.py
@@ -24,11 +24,6 @@
 NS_B = -4.775
 NS_C = 2.0315
 EPS_NORM = 1e-06
-HIGH = lax.Precision.HIGH
-
-
-def f32dot(a, b, dims=(((1,), (0,)), ((), ()))):
-    return lax.dot_general(a, b, dims, precision=HIGH, preferred_element_type=F32)
 
 
 def bdot(a, b, dims=(((1,), (0,)), ((), ()))):
@@ -41,8 +36,8 @@
 
 def body(
     lens_h, tissue_h, feat_h, cot_h, dk_h, gain_h, wu_h, bias_h, wd_h, scale_h,
-    out_ref, gout_ref, mu_ref, md_ref,
-    lens, tissue, feat, cot, dk, gain1, bias1, scale1, pieces, piece_in, t24, wg, wm, rim, halo, frame, mixed, inv_s, left, right,
+    tok_ref, muon_ref,
+    lens, tissue, feat, cot, dk, gain1, bias1, scale1, t96, wg, wm, rim, halo, frame, mixed, inv_s, left, right,
     zs, zr, bs, br, gs, grv, gf, gb, rx, ty, ry, grow, ga, gm16, hg, nb, ct, chd, frame2, xo,
     ss, rs, ls,
 ):
@@ -82,7 +77,7 @@
     fetches = {}
     for n, (name, src, dst) in enumerate(
         (
-            ("wu", wu_h, pieces.at[0]), ("wd", wd_h, pieces.at[1]), ("lens", lens_h, lens),
+            ("wu", wu_h, wg.at[0, y, x, c]), ("wd", wd_h, wg.at[1, y, x, c]), ("lens", lens_h, lens),
             ("feat", feat_h, feat), ("tissue", tissue_h, tissue), ("dk", dk_h, dk), ("gain", gain_h, gain1),
             ("scale", scale_h, scale1), ("cot", cot_h, cot), ("bias", bias_h, bias1),
         )
@@ -123,8 +118,43 @@
     fetches["wd"].wait()
     pl.semaphore_wait(bar, expected + 4 * ((NZ - o) // NZ) + lax.rem(o, 2))
 
-    s_piece = sem_ids(1)
-    send(pieces.at[1 - c], piece_in, s_piece, (sib, o))
+    near = (1, 7, 2, 6, 3, 5, 4)
+    far = near[::-1]
+
+    def row_of(k):
+        return lax.rem(y + NY - k, NY)
+
+    def share_x(at, row, sem):
+        for k in range(1, NX):
+            send(at(row, x), at(row, x), sem + k - 1, (tile_at(y, lax.rem(x + k, NX)), o))
+
+    def gather_start(at, s_y, s_x):
+        for k in far:
+            send(at(y, x), at(y, x), s_y + k - 1, (tile_at(lax.rem(y + k, NY), x), o))
+        share_x(at, y, s_x)
+
+    def gather_relay(at, s_y, s_x, ks):
+        for k in ks:
+            row = row_of(k)
+            arrived(at(row, x), s_y + k - 1)
+            share_x(at, row, s_x + 3 * k)
+
+    def gather_row(at, s_x, k):
+        row = row_of(k)
+        for n in range(1, NX):
+            arrived(at(row, lax.rem(x + NX - n, NX)), s_x + 3 * k + n - 1)
+        return row
+
+    def weight_at(row, col):
+        return wg.at[:, row, col, c]
+
+    def grad_at(row, col):
+        return ga.at[row, col]
+
+    s_wy = sem_ids(NY - 1)
+    s_wx = sem_ids(3 * NY)
+    s_ws = sem_ids(NY)
+    gather_start(weight_at, s_wy, s_wx)
 
     fetches["lens"].wait()
     fetches["feat"].wait()
@@ -137,47 +167,6 @@
     s_halo = sem_ids(2)
     send(rim.at[1], halo.at[0], s_halo, (up_t, o))
     send(rim.at[0], halo.at[1], s_halo + 1, (dn_t, o))
-
-    arrived(piece_in, s_piece)
-    mine = pieces[c].astype(F32)
-    other = piece_in[...].astype(F32)
-    t24[0:12, :] = jnp.where(c == 0, mine, other)
-    t24[12:24, :] = jnp.where(c == 0, other, mine)
-    wg[c, y, x] = t24[...].astype(BF16)
-
-    near = (1, 7, 2, 6, 3, 5, 4)
-    far = near[::-1]
-
-    def row_of(k):
-        return lax.rem(y + NY - k, NY)
-
-    def share_x(buf, row, sem):
-        for k in range(1, NX):
-            send(buf.at[row, x], buf.at[row, x], sem + k - 1, (tile_at(y, lax.rem(x + k, NX)), o))
-
-    def gather_start(buf, s_y, s_x):
-        for k in far:
-            send(buf.at[y, x], buf.at[y, x], s_y + k - 1, (tile_at(lax.rem(y + k, NY), x), o))
-        share_x(buf, y, s_x)
-
-    def gather_relay(buf, s_y, s_x, ks):
-        for k in ks:
-            row = row_of(k)
-            arrived(buf.at[row, x], s_y + k - 1)
-            share_x(buf, row, s_x + 3 * k)
-
-    def gather_row(buf, s_x, k):
-        row = row_of(k)
-        for n in range(1, NX):
-            arrived(buf.at[row, lax.rem(x + NX - n, NX)], s_x + 3 * k + n - 1)
-        return row
-
-    s_wy = sem_ids(NY - 1)
-    s_wx = sem_ids(3 * NY)
-    s_ws = sem_ids(NY)
-    wg_c = wg.at[c]
-    wg_o = wg.at[1 - c]
-    gather_start(wg_c, s_wy, s_wx)
 
     for name in ("tissue", "dk", "gain", "scale", "cot", "bias"):
         fetches[name].wait()
@@ -222,9 +211,9 @@
         lax.fori_loop(0, CH, chunk, 0)
 
     conv_half(0)
-    gather_relay(wg_c, s_wy, s_wx, near[:4])
+    gather_relay(weight_at, s_wy, s_wx, near[:4])
     conv_half(1)
-    gather_relay(wg_c, s_wy, s_wx, near[4:6])
+    gather_relay(weight_at, s_wy, s_wx, near[4:6])
 
     for q in range(4):
         rows = slice(64 * q, 64 * q + 64)
@@ -237,19 +226,26 @@
         inv_s[rows, :] = inv
         left[0, rows, :] = (centred * gain).astype(BF16)
 
-    gather_relay(wg_c, s_wy, s_wx, near[6:])
-
-    def take(m, row):
-        wm[m, row] = wg[m, row].astype(F32).reshape(96, HID).astype(BF16)
-
+    gather_relay(weight_at, s_wy, s_wx, near[6:])
+
+    def take(k):
+        row = row_of(k)
+        arrived(wg.at[:, row, :, 1 - c], s_ws + k)
+        for m in range(2):
+            for col in range(NX):
+                for core in range(2):
+                    first = 24 * col + 12 * core
+                    t96[m, first : first + 12, :] = wg[m, row, col, core].astype(F32)
+            wm[m, row] = t96[m].astype(BF16)
+
+    last = None
     for k in (0,) + near:
-        row = gather_row(wg_c, s_wx, k)
-        send(wg_c.at[row], wg_c.at[row], s_ws + k, (sib, o))
-        take(c, row)
-    for k in (0,) + near:
-        row = row_of(k)
-        arrived(wg_o.at[row], s_ws + k)
-        take(1 - c, row)
+        row = gather_row(weight_at, s_wx, k)
+        send(wg.at[:, row, :, c], wg.at[:, row, :, c], s_ws + k, (sib, o))
+        if last is not None:
+            take(last)
+        last = k
+    take(last)
 
     up_w = wm[0].reshape(D, HID)
     down_w = wm[1].reshape(D, HID)
@@ -260,9 +256,11 @@
     slope = phi + hidden * jnp.exp(-0.5 * hidden * hidden) * INV_ROOT_TAU
     right[0] = (grad_act * slope).astype(BF16)
 
-    s_g = sem_ids(1)
+    s_g = sem_ids(NY)
     gs[...] = bdot(left[1 - c], right[1 - c], TN_DIMS).reshape(NY, NX, RB, HID).astype(BF16)
-    send(gs, grv, s_g, (sib, o))
+    for k in far + (0,):
+        row = lax.rem(y + k, NY)
+        send(gs.at[row], grv.at[row], s_g + k, (sib, o))
 
     def scatter_z(value, buf, slots, s0):
         buf[...] = value.reshape(NZ, OWN_TOK, D).astype(BF16)
@@ -284,9 +282,9 @@
 
     s_rx = sem_ids(3 * NY)
     s_ry = sem_ids(NY - 1)
-    arrived(grv, s_g)
     for k in far + (0,):
         row = lax.rem(y + k, NY)
+        arrived(grv.at[row], s_g + k)
         pair = gf[row] + grv[row].astype(F32)
         gf[row] = pair
         gb[row] = pair.astype(BF16)
@@ -311,7 +309,7 @@
     ga[y, x] = total.astype(BF16)
     s_gy = sem_ids(NY - 1)
     s_gx = sem_ids(3 * NY)
-    gather_start(ga, s_gy, s_gx)
+    gather_start(grad_at, s_gy, s_gx)
 
     grad_normed = scatter_z_sum(zs, zr, s_z)
     own_rows = pl.ds(pl.multiple_of(o * OWN_TOK, OWN_TOK), OWN_TOK)
@@ -350,7 +348,7 @@
     for ch in range(CH):
         frame2[ch, 3:7, 3:11, :] = grad_mixed[:, 128 * ch : 128 * ch + 128].reshape(4, 8, 128)
 
-    gather_relay(ga, s_gy, s_gx, near[:4])
+    gather_relay(grad_at, s_gy, s_gx, near[:4])
 
     def put_before(block):
         rows3 = block.astype(F32)[8:32]
@@ -362,7 +360,7 @@
         for ch in range(CH):
             frame2[ch, 7:10, 3:11, :] = rows3[:, 128 * ch : 128 * ch + 128].reshape(3, 8, 128)
 
-    gather_relay(ga, s_gy, s_gx, near[4:])
+    gather_relay(grad_at, s_gy, s_gx, near[4:])
     arrived(nb.at[0], s_h)
     arrived(nb.at[1], s_h + 1)
 
@@ -408,7 +406,7 @@
                 w = dk[6 - i, 6 - j : 7 - j, lanes].reshape(1, 1, 128)
                 acc = acc + w * frame2[ch, i : i + 4, j : j + 8, :]
         res = cot[own_rows, lanes].astype(F32) + acc.reshape(OWN_TOK, 128)
-        gout_ref[:, lanes] = jnp.where(own_live, res, 0.0).astype(BF16)
+        tok_ref[1, :, lanes] = jnp.where(own_live, res, 0.0).astype(BF16)
         return 0
 
     lax.fori_loop(0, CH, chunk2, 0)
@@ -416,11 +414,11 @@
     branch = scatter_z_sum(bs, br, s_b)
     own_keep = jnp.where(own_live, tissue[o // 2], 0).astype(F32)
     res = feat[own_rows, :].astype(F32) + (own_keep * scale) * branch
-    out_ref[...] = jnp.where(own_live, res, 0.0).astype(BF16)
+    tok_ref[0] = jnp.where(own_live, res, 0.0).astype(BF16)
 
     def gram_of(ks):
         for n, k in enumerate(ks):
-            row = gather_row(ga, s_gx, k)
+            row = gather_row(grad_at, s_gx, k)
             gm16[n] = ga[row].astype(F32).reshape(96, HID).astype(BF16)
         g16 = gm16[0 : len(ks)].reshape(96 * len(ks), HID)
         return bdot(g16, g16, TN_DIMS)
@@ -434,18 +432,24 @@
     root = lax.rsqrt(norm2 + EPS_NORM)
     gram = gram * (root * root)
 
-    def poly(a):
-        return NS_A * eye + NS_B * a + NS_C * f32dot(a, a)
-
-    p0 = poly(gram)
-    gram1 = f32dot(f32dot(gram, p0), p0)
-    p1 = poly(gram1)
-    xo[c] = f32dot(f32dot(grow[...] * root, p0), p1)
+    def times(a, b):
+        return bdot(a.astype(BF16), b)
+
+    def residue(a):
+        a16 = a.astype(BF16)
+        return (NS_B * a + NS_C * bdot(a16, a16)).astype(BF16)
+
+    q0 = residue(gram)
+    first = NS_A * gram + times(gram, q0)
+    q1 = residue(NS_A * first + times(first, q0))
+    ortho = grow[...] * root
+    ortho = NS_A * ortho + times(ortho, q0)
+    xo[c] = NS_A * ortho + times(ortho, q1)
     s_x = sem_ids(1)
     send(xo.at[c], xo.at[c], s_x, (sib, o))
     arrived(xo.at[1 - c], s_x)
-    mu_ref[...] = jnp.where(c == 0, xo[0, 0:12, :], xo[0, 12:24, :])
-    md_ref[...] = jnp.where(c == 0, xo[1, 0:12, :], xo[1, 12:24, :])
+    for m in range(2):
+        muon_ref[m] = jnp.where(c == 0, xo[m, 0:12, :], xo[m, 12:24, :])
 
     for cp in sent:
         cp.wait_send()
@@ -467,10 +471,8 @@
         pltpu.VMEM((D,), F32),
         pltpu.VMEM((HID,), F32),
         pltpu.VMEM((D,), F32),
-        pltpu.VMEM((2, 12, HID), BF16),
-        pltpu.VMEM((12, HID), BF16),
-        pltpu.VMEM((24, HID), F32),
-        pltpu.VMEM((2,) + block4, BF16),
+        pltpu.VMEM((2, 96, HID), F32),
+        pltpu.VMEM((2, NY, NX, 2, 12, HID), BF16),
         pltpu.VMEM((2, NY, 96, HID), BF16),
         pltpu.VMEM((2, 24, D), BF16),
         pltpu.VMEM((2, 24, D), BF16),
@@ -506,13 +508,11 @@
     outs = pl.pallas_call(
         body,
         out_shape=(
-            jax.ShapeDtypeStruct((OWN_TOK, D), BF16),
-            jax.ShapeDtypeStruct((OWN_TOK, D), BF16),
-            jax.ShapeDtypeStruct((12, HID), F32),
-            jax.ShapeDtypeStruct((12, HID), F32),
+            jax.ShapeDtypeStruct((2, OWN_TOK, D), BF16),
+            jax.ShapeDtypeStruct((2, 12, HID), F32),
         ),
         in_specs=[hbm] * 10,
-        out_specs=(vmem,) * 4,
+        out_specs=(vmem,) * 2,
         scratch_shapes=scratch,
         compiler_params=pltpu.CompilerParams(
             collective_id=0, has_side_effects=True, vmem_limit_bytes=62 << 20
@@ -529,12 +529,12 @@
         weight_down.T,
         layer_scale,
     )
-    block_out, grad_features, muon_up, muon_down_t = outs
+    tokens, muon = outs
     return (
-        block_out.reshape(4, 8, D),
-        grad_features.reshape(4, 8, D),
-        muon_up,
-        muon_down_t.T,
+        tokens[0].reshape(4, 8, D),
+        tokens[1].reshape(4, 8, D),
+        muon[0],
+        muon[1].T,
     )
 
 

time: 70.3 us -> 69 us (0.982)
  local copies, waits for them, and re-layouts: 3.53 us -> 2.1 us
    unnamed x10 -> x2, local copies, waits for them, and re-layouts: 3.53 us -> 0.01 us
    another operation x0 -> x1, local copies, waits for them, and re-layouts: none -> 1.47 us  [shards(): tokens[1].reshape(4, 8, D)]
where the time goes in v4:
time: 69 us; the launch traced here: 68.8 us
  Pallas kernels  66 us (96%)
  local copies, waits for them, and re-layouts  2.1 us (3%)
    pallas_call x1, Pallas kernels, shards(): pl.pallas_call(body, out_shape=(jax.ShapeDtypeStruct((2, OWN_TOK, D), BF1...  66 us
    another operation x1, local copies, waits for them, and re-layouts, shards(): tokens[1].reshape(4, 8, D)  1.47 us

profile of v4, /device:TPU:1, one launch (start us, length us, event | category | flops | bytes accessed | tf_op | source)
XLA Modules:
  0.0 68.8 jit_solution(11132785074694279318)
XLA Ops:
  0.6 66.0 %shard_map.129 = (bf16[2,32,768]{2,1,0:T(8,128)(2,1)}, f32[2,12,384]{2,1,0:T(8,128)}) custom-call(s32[64]{0:T(128)} %lens_h.1, s32[4]{0:T(128)} %bitcast.17, bf16[256,768]{1,0:T(8,128)(2,1)} %bitcast.14, bf16[256,768]{1,0:T(8,128)(2,1)} %bitcast.15, f32[7,7,768]{2,1,0:T(8,128)} %dk_h.1, f32[768]{0:T(1024)} %gain_h.1, bf16[12,384]{1,0:T(8,128)(2,1)} %wu_h.1, ...), custom_call_target="tpu_custom_call" | custom-call | tf_op jit(solution)/shard_map/pallas_call | solution.py:508
  66.7 0.0 copy-start
  66.7 1.5 %slice_bitcast_fusion = (bf16[4,8,768]{2,1,0:T(8,128)(2,1)}, bf16[4,8,768]{2,1,0:T(8,128)(2,1)}) fusion(bf16[2,32,768]{2,1,0:T(8,128)(2,1)} %get-tuple-element.6), kind=kLoop, calls=%fused_computation | loop fusion | bytes 196608 | tf_op jit(solution)/shard_map/reshape;squeeze | solution.py:535
  68.2 0.0 copy-done
  68.2 0.6 slice_bitcast_fusion.2
Async XLA Ops:
  66.7 1.5 %copy-start = (f32[2,12,384]{2,1,0:T(8,128)S(1)}, f32[2,12,384]{2,1,0:T(8,128)}, u32[]{:S(2)}) copy-start(f32[2,12,384]{2,1,0:T(8,128)} %get-tuple-element.7) | copy-start | bytes 110596

commit v5 on v4

--- a/solution.py
+++ b/solution.py
@@ -37,7 +37,7 @@
 def body(
     lens_h, tissue_h, feat_h, cot_h, dk_h, gain_h, wu_h, bias_h, wd_h, scale_h,
     tok_ref, muon_ref,
-    lens, tissue, feat, cot, dk, gain1, bias1, scale1, t96, wg, wm, rim, halo, frame, mixed, inv_s, left, right,
+    lens, tissue, feat, cot, dk, gain1, bias1, scale1, pieces, piece_in, t24, wg, wm, rim, halo, frame, mixed, inv_s, left, right,
     zs, zr, bs, br, gs, grv, gf, gb, rx, ty, ry, grow, ga, gm16, hg, nb, ct, chd, frame2, xo,
     ss, rs, ls,
 ):
@@ -77,7 +77,7 @@
     fetches = {}
     for n, (name, src, dst) in enumerate(
         (
-            ("wu", wu_h, wg.at[0, y, x, c]), ("wd", wd_h, wg.at[1, y, x, c]), ("lens", lens_h, lens),
+            ("wu", wu_h, pieces.at[0]), ("wd", wd_h, pieces.at[1]), ("lens", lens_h, lens),
             ("feat", feat_h, feat), ("tissue", tissue_h, tissue), ("dk", dk_h, dk), ("gain", gain_h, gain1),
             ("scale", scale_h, scale1), ("cot", cot_h, cot), ("bias", bias_h, bias1),
         )
@@ -118,6 +118,9 @@
     fetches["wd"].wait()
     pl.semaphore_wait(bar, expected + 4 * ((NZ - o) // NZ) + lax.rem(o, 2))
 
+    s_piece = sem_ids(1)
+    send(pieces.at[1 - c], piece_in, s_piece, (sib, o))
+
     near = (1, 7, 2, 6, 3, 5, 4)
     far = near[::-1]
 
@@ -146,7 +149,7 @@
         return row
 
     def weight_at(row, col):
-        return wg.at[:, row, col, c]
+        return wg.at[c, row, col]
 
     def grad_at(row, col):
         return ga.at[row, col]
@@ -154,8 +157,6 @@
     s_wy = sem_ids(NY - 1)
     s_wx = sem_ids(3 * NY)
     s_ws = sem_ids(NY)
-    gather_start(weight_at, s_wy, s_wx)
-
     fetches["lens"].wait()
     fetches["feat"].wait()
     length = lens[t]
@@ -167,6 +168,14 @@
     s_halo = sem_ids(2)
     send(rim.at[1], halo.at[0], s_halo, (up_t, o))
     send(rim.at[0], halo.at[1], s_halo + 1, (dn_t, o))
+
+    arrived(piece_in, s_piece)
+    mine = pieces[c].astype(F32)
+    other = piece_in[...].astype(F32)
+    t24[0:12, :] = jnp.where(c == 0, mine, other)
+    t24[12:24, :] = jnp.where(c == 0, other, mine)
+    wg[c, y, x] = t24[...].astype(BF16)
+    gather_start(weight_at, s_wy, s_wx)
 
     for name in ("tissue", "dk", "gain", "scale", "cot", "bias"):
         fetches[name].wait()
@@ -228,24 +237,22 @@
 
     gather_relay(weight_at, s_wy, s_wx, near[6:])
 
-    def take(k):
-        row = row_of(k)
-        arrived(wg.at[:, row, :, 1 - c], s_ws + k)
-        for m in range(2):
-            for col in range(NX):
-                for core in range(2):
-                    first = 24 * col + 12 * core
-                    t96[m, first : first + 12, :] = wg[m, row, col, core].astype(F32)
-            wm[m, row] = t96[m].astype(BF16)
+    def take(m, k):
+        wm[m, row_of(k)] = wg[m, row_of(k)].astype(F32).reshape(96, HID).astype(BF16)
+
+    def take_other(k):
+        arrived(wg.at[1 - c, row_of(k)], s_ws + k)
+        take(1 - c, k)
 
     last = None
     for k in (0,) + near:
         row = gather_row(weight_at, s_wx, k)
-        send(wg.at[:, row, :, c], wg.at[:, row, :, c], s_ws + k, (sib, o))
+        send(wg.at[c, row], wg.at[c, row], s_ws + k, (sib, o))
+        take(c, k)
         if last is not None:
-            take(last)
+            take_other(last)
         last = k
-    take(last)
+    take_other(last)
 
     up_w = wm[0].reshape(D, HID)
     down_w = wm[1].reshape(D, HID)
@@ -311,6 +318,8 @@
     s_gx = sem_ids(3 * NY)
     gather_start(grad_at, s_gy, s_gx)
 
+    gather_relay(grad_at, s_gy, s_gx, near[:4])
+
     grad_normed = scatter_z_sum(zs, zr, s_z)
     own_rows = pl.ds(pl.multiple_of(o * OWN_TOK, OWN_TOK), OWN_TOK)
     own_live = length > o // 2
@@ -348,8 +357,39 @@
     for ch in range(CH):
         frame2[ch, 3:7, 3:11, :] = grad_mixed[:, 128 * ch : 128 * ch + 128].reshape(4, 8, 128)
 
-    gather_relay(grad_at, s_gy, s_gx, near[:4])
-
+    gather_relay(grad_at, s_gy, s_gx, near[4:])
+
+    def gram_of(ks):
+        for n, k in enumerate(ks):
+            row = gather_row(grad_at, s_gx, k)
+            gm16[n] = ga[row].astype(F32).reshape(96, HID).astype(BF16)
+        g16 = gm16[0 : len(ks)].reshape(96 * len(ks), HID)
+        return bdot(g16, g16, TN_DIMS)
+
+    gram = gram_of((0,) + near[:4]) + gram_of(near[4:])
+    eye = (
+        lax.broadcasted_iota(jnp.int32, (HID, HID), 0) == lax.broadcasted_iota(jnp.int32, (HID, HID), 1)
+    ).astype(F32)
+
+    norm2 = jnp.sum(jnp.sum(gram * eye, axis=0, keepdims=True), axis=1, keepdims=True)
+    root = lax.rsqrt(norm2 + EPS_NORM)
+    gram = gram * (root * root)
+
+    def times(a, b):
+        return bdot(a.astype(BF16), b)
+
+    def residue(a):
+        a16 = a.astype(BF16)
+        return (NS_B * a + NS_C * bdot(a16, a16)).astype(BF16)
+
+    q0 = residue(gram)
+    first = NS_A * gram + times(gram, q0)
+    q1 = residue(NS_A * first + times(first, q0))
+    ortho = grow[...] * root
+    ortho = NS_A * ortho + times(ortho, q0)
+    xo[c] = NS_A * ortho + times(ortho, q1)
+    s_x = sem_ids(1)
+    send(xo.at[c], xo.at[c], s_x, (sib, o))
     def put_before(block):
         rows3 = block.astype(F32)[8:32]
         for ch in range(CH):
@@ -360,7 +400,6 @@
         for ch in range(CH):
             frame2[ch, 7:10, 3:11, :] = rows3[:, 128 * ch : 128 * ch + 128].reshape(3, 8, 128)
 
-    gather_relay(grad_at, s_gy, s_gx, near[4:])
     arrived(nb.at[0], s_h)
     arrived(nb.at[1], s_h + 1)
 
@@ -416,37 +455,6 @@
     res = feat[own_rows, :].astype(F32) + (own_keep * scale) * branch
     tok_ref[0] = jnp.where(own_live, res, 0.0).astype(BF16)
 
-    def gram_of(ks):
-        for n, k in enumerate(ks):
-            row = gather_row(grad_at, s_gx, k)
-            gm16[n] = ga[row].astype(F32).reshape(96, HID).astype(BF16)
-        g16 = gm16[0 : len(ks)].reshape(96 * len(ks), HID)
-        return bdot(g16, g16, TN_DIMS)
-
-    gram = gram_of((0,) + near[:4]) + gram_of(near[4:])
-    eye = (
-        lax.broadcasted_iota(jnp.int32, (HID, HID), 0) == lax.broadcasted_iota(jnp.int32, (HID, HID), 1)
-    ).astype(F32)
-
-    norm2 = jnp.sum(jnp.sum(gram * eye, axis=0, keepdims=True), axis=1, keepdims=True)
-    root = lax.rsqrt(norm2 + EPS_NORM)
-    gram = gram * (root * root)
-
-    def times(a, b):
-        return bdot(a.astype(BF16), b)
-
-    def residue(a):
-        a16 = a.astype(BF16)
-        return (NS_B * a + NS_C * bdot(a16, a16)).astype(BF16)
-
-    q0 = residue(gram)
-    first = NS_A * gram + times(gram, q0)
-    q1 = residue(NS_A * first + times(first, q0))
-    ortho = grow[...] * root
-    ortho = NS_A * ortho + times(ortho, q0)
-    xo[c] = NS_A * ortho + times(ortho, q1)
-    s_x = sem_ids(1)
-    send(xo.at[c], xo.at[c], s_x, (sib, o))
     arrived(xo.at[1 - c], s_x)
     for m in range(2):
         muon_ref[m] = jnp.where(c == 0, xo[m, 0:12, :], xo[m, 12:24, :])
@@ -471,8 +479,10 @@
         pltpu.VMEM((D,), F32),
         pltpu.VMEM((HID,), F32),
         pltpu.VMEM((D,), F32),
-        pltpu.VMEM((2, 96, HID), F32),
-        pltpu.VMEM((2, NY, NX, 2, 12, HID), BF16),
+        pltpu.VMEM((2, 12, HID), BF16),
+        pltpu.VMEM((12, HID), BF16),
+        pltpu.VMEM((24, HID), F32),
+        pltpu.VMEM((2,) + block4, BF16),
         pltpu.VMEM((2, NY, 96, HID), BF16),
         pltpu.VMEM((2, 24, D), BF16),
         pltpu.VMEM((2, 24, D), BF16),

time: 69 us -> 65.7 us (0.952)
  Pallas kernels: 66 us -> 62.8 us
    pallas_call x1, Pallas kernels: 66 us -> 62.8 us  [shards(): pl.pallas_call(body, out_shape=(jax.ShapeDtypeStruct((2, OWN_TOK, D), BF1...]
where the time goes in v5:
time: 65.7 us; the launch traced here: 65.5 us
  Pallas kernels  62.8 us (96%)
  local copies, waits for them, and re-layouts  2.1 us (3%)
    pallas_call x1, Pallas kernels, shards(): pl.pallas_call(body, out_shape=(jax.ShapeDtypeStruct((2, OWN_TOK, D), BF1...  62.8 us
    another operation x1, local copies, waits for them, and re-layouts, shards(): tokens[1].reshape(4, 8, D)  1.47 us

profile of v5, /device:TPU:1, one launch (start us, length us, event | category | flops | bytes accessed | tf_op | source)
XLA Modules:
  0.0 65.5 jit_solution(9258103807158673871)
XLA Ops:
  0.6 62.8 %shard_map.129 = (bf16[2,32,768]{2,1,0:T(8,128)(2,1)}, f32[2,12,384]{2,1,0:T(8,128)}) custom-call(s32[64]{0:T(128)} %lens_h.1, s32[4]{0:T(128)} %bitcast.17, bf16[256,768]{1,0:T(8,128)(2,1)} %bitcast.14, bf16[256,768]{1,0:T(8,128)(2,1)} %bitcast.15, f32[7,7,768]{2,1,0:T(8,128)} %dk_h.1, f32[768]{0:T(1024)} %gain_h.1, bf16[12,384]{1,0:T(8,128)(2,1)} %wu_h.1, ...), custom_call_target="tpu_custom_call" | custom-call | tf_op jit(solution)/shard_map/pallas_call | solution.py:518
  63.4 0.0 copy-start
  63.4 1.5 %slice_bitcast_fusion = (bf16[4,8,768]{2,1,0:T(8,128)(2,1)}, bf16[4,8,768]{2,1,0:T(8,128)(2,1)}) fusion(bf16[2,32,768]{2,1,0:T(8,128)(2,1)} %get-tuple-element.6), kind=kLoop, calls=%fused_computation | loop fusion | bytes 196608 | tf_op jit(solution)/shard_map/reshape;squeeze | solution.py:545
  64.9 0.0 copy-done
  64.9 0.6 slice_bitcast_fusion.2
Async XLA Ops:
  63.4 1.5 %copy-start = (f32[2,12,384]{2,1,0:T(8,128)S(1)}, f32[2,12,384]{2,1,0:T(8,128)}, u32[]{:S(2)}) copy-start(f32[2,12,384]{2,1,0:T(8,128)} %get-tuple-element.7) | copy-start | bytes 110596

commit v6 on v5

--- a/solution.py
+++ b/solution.py
@@ -38,7 +38,7 @@
     lens_h, tissue_h, feat_h, cot_h, dk_h, gain_h, wu_h, bias_h, wd_h, scale_h,
     tok_ref, muon_ref,
     lens, tissue, feat, cot, dk, gain1, bias1, scale1, pieces, piece_in, t24, wg, wm, rim, halo, frame, mixed, inv_s, left, right,
-    zs, zr, bs, br, gs, grv, gf, gb, rx, ty, ry, grow, ga, gm16, hg, nb, ct, chd, frame2, xo,
+    zs, zr, bs, br, left_in, right_in, gf, gb, rx, ty, ry, grow, ga, gm16, hg, nb, ct, chd, frame2, xo,
     ss, rs, ls,
 ):
     t = lax.axis_index("tile")
@@ -132,7 +132,7 @@
             send(at(row, x), at(row, x), sem + k - 1, (tile_at(y, lax.rem(x + k, NX)), o))
 
     def gather_start(at, s_y, s_x):
-        for k in far:
+        for k in near:
             send(at(y, x), at(y, x), s_y + k - 1, (tile_at(lax.rem(y + k, NY), x), o))
         share_x(at, y, s_x)
 
@@ -236,6 +236,8 @@
         left[0, rows, :] = (centred * gain).astype(BF16)
 
     gather_relay(weight_at, s_wy, s_wx, near[6:])
+    s_l = sem_ids(2)
+    send(left.at[1 - c], left_in, s_l, (sib, o))
 
     def take(m, k):
         wm[m, row_of(k)] = wg[m, row_of(k)].astype(F32).reshape(96, HID).astype(BF16)
@@ -263,11 +265,7 @@
     slope = phi + hidden * jnp.exp(-0.5 * hidden * hidden) * INV_ROOT_TAU
     right[0] = (grad_act * slope).astype(BF16)
 
-    s_g = sem_ids(NY)
-    gs[...] = bdot(left[1 - c], right[1 - c], TN_DIMS).reshape(NY, NX, RB, HID).astype(BF16)
-    for k in far + (0,):
-        row = lax.rem(y + k, NY)
-        send(gs.at[row], grv.at[row], s_g + k, (sib, o))
+    send(right.at[1 - c], right_in, s_l + 1, (sib, o))
 
     def scatter_z(value, buf, slots, s0):
         buf[...] = value.reshape(NZ, OWN_TOK, D).astype(BF16)
@@ -284,17 +282,18 @@
 
     s_z = sem_ids(NZ - 1)
     s_b = sem_ids(NZ - 1)
-    gf[...] = bdot(left[c], right[c], TN_DIMS).reshape(NY, NX, RB, HID)
     scatter_z(bdot(right[0], up_w, NT_DIMS), zs, zr, s_z)
+    arrived(left_in, s_l)
+    arrived(right_in, s_l + 1)
+    both = bdot(left[c], right[c], TN_DIMS) + bdot(left_in[...], right_in[...], TN_DIMS)
+    both = both.reshape(NY, NX, RB, HID)
+    gf[...] = both
+    gb[...] = both.astype(BF16)
 
     s_rx = sem_ids(3 * NY)
     s_ry = sem_ids(NY - 1)
     for k in far + (0,):
         row = lax.rem(y + k, NY)
-        arrived(grv.at[row], s_g + k)
-        pair = gf[row] + grv[row].astype(F32)
-        gf[row] = pair
-        gb[row] = pair.astype(BF16)
         for n in range(1, NX):
             col = lax.rem(x + n, NX)
             send(gb.at[row, col], rx.at[row, n - 1], s_rx + 3 * k + n - 1, (tile_at(y, col), o))
@@ -495,8 +494,8 @@
         pltpu.VMEM((NZ - 1, OWN_TOK, D), BF16),
         pltpu.VMEM((NZ, OWN_TOK, D), BF16),
         pltpu.VMEM((NZ - 1, OWN_TOK, D), BF16),
-        pltpu.VMEM(block4, BF16),
-        pltpu.VMEM(block4, BF16),
+        pltpu.VMEM((TOK, D), BF16),
+        pltpu.VMEM((TOK, HID), BF16),
         pltpu.VMEM(block4, F32),
         pltpu.VMEM(block4, BF16),
         pltpu.VMEM((NY, NX - 1, RB, HID), BF16),

time: 65.7 us -> 65.1 us (level)
  no operation moved by 1% of the time
where the time goes in v6:
time: 65.1 us; the launch traced here: 64.9 us
  Pallas kernels  62.2 us (96%)
  local copies, waits for them, and re-layouts  2.1 us (3%)
    pallas_call x1, Pallas kernels, shards(): pl.pallas_call(body, out_shape=(jax.ShapeDtypeStruct((2, OWN_TOK, D), BF1...  62.2 us
    another operation x1, local copies, waits for them, and re-layouts, shards(): tokens[1].reshape(4, 8, D)  1.47 us

profile of v6, /device:TPU:1, one launch (start us, length us, event | category | flops | bytes accessed | tf_op | source)
XLA Modules:
  0.0 64.9 jit_solution(7087559434381833704)
XLA Ops:
  0.6 62.2 %shard_map.129 = (bf16[2,32,768]{2,1,0:T(8,128)(2,1)}, f32[2,12,384]{2,1,0:T(8,128)}) custom-call(s32[64]{0:T(128)} %lens_h.1, s32[4]{0:T(128)} %bitcast.17, bf16[256,768]{1,0:T(8,128)(2,1)} %bitcast.14, bf16[256,768]{1,0:T(8,128)(2,1)} %bitcast.15, f32[7,7,768]{2,1,0:T(8,128)} %dk_h.1, f32[768]{0:T(1024)} %gain_h.1, bf16[12,384]{1,0:T(8,128)(2,1)} %wu_h.1, ...), custom_call_target="tpu_custom_call" | custom-call | tf_op jit(solution)/shard_map/pallas_call | solution.py:517
  62.8 0.0 copy-start
  62.8 1.5 %slice_bitcast_fusion = (bf16[4,8,768]{2,1,0:T(8,128)(2,1)}, bf16[4,8,768]{2,1,0:T(8,128)(2,1)}) fusion(bf16[2,32,768]{2,1,0:T(8,128)(2,1)} %get-tuple-element.6), kind=kLoop, calls=%fused_computation | loop fusion | bytes 196608 | tf_op jit(solution)/shard_map/reshape;squeeze | solution.py:544
  64.3 0.0 copy-done
  64.3 0.6 slice_bitcast_fusion.2
Async XLA Ops:
  62.8 1.5 %copy-start = (f32[2,12,384]{2,1,0:T(8,128)S(1)}, f32[2,12,384]{2,1,0:T(8,128)}, u32[]{:S(2)}) copy-start(f32[2,12,384]{2,1,0:T(8,128)} %get-tuple-element.7) | copy-start | bytes 110596

commit v7 on v6

--- a/solution.py
+++ b/solution.py
@@ -54,6 +54,7 @@
 
     counter = [0]
     sent = []
+    along_z = []
 
     def sem_ids(n):
         first = counter[0]
@@ -70,6 +71,11 @@
         cp = copy(src, dst, sem, dev)
         cp.start()
         sent.append(cp)
+
+    def drain():
+        for cp in sent:
+            cp.wait_send()
+        sent.clear()
 
     def arrived(dst, sem):
         copy(dst, dst, sem, (t, o)).wait_recv()
@@ -219,10 +225,10 @@
 
         lax.fori_loop(0, CH, chunk, 0)
 
+    gather_relay(weight_at, s_wy, s_wx, near[:2])
     conv_half(0)
-    gather_relay(weight_at, s_wy, s_wx, near[:4])
+    gather_relay(weight_at, s_wy, s_wx, near[2:6])
     conv_half(1)
-    gather_relay(weight_at, s_wy, s_wx, near[4:6])
 
     for q in range(4):
         rows = slice(64 * q, 64 * q + 64)
@@ -271,7 +277,9 @@
         buf[...] = value.reshape(NZ, OWN_TOK, D).astype(BF16)
         for k in far:
             dest = lax.rem(o + k, NZ)
-            send(buf.at[dest], slots.at[k - 1], s0 + k - 1, (t, dest))
+            cp = copy(buf.at[dest], slots.at[k - 1], s0 + k - 1, (t, dest))
+            cp.start()
+            along_z.append(cp)
 
     def scatter_z_sum(buf, slots, s0):
         total = buf[o].astype(F32)
@@ -290,6 +298,9 @@
     gf[...] = both
     gb[...] = both.astype(BF16)
 
+    early = list(sent)
+    sent.clear()
+
     s_rx = sem_ids(3 * NY)
     s_ry = sem_ids(NY - 1)
     for k in far + (0,):
@@ -298,6 +309,8 @@
             col = lax.rem(x + n, NX)
             send(gb.at[row, col], rx.at[row, n - 1], s_rx + 3 * k + n - 1, (tile_at(y, col), o))
     scatter_z(bdot(right[1], down_w, NT_DIMS), bs, br, s_b)
+    for cp in early:
+        cp.wait_send()
     total = None
     for k in far + (0,):
         row = lax.rem(y + k, NY)
@@ -315,7 +328,11 @@
     ga[y, x] = total.astype(BF16)
     s_gy = sem_ids(NY - 1)
     s_gx = sem_ids(3 * NY)
+    early = list(sent)
+    sent.clear()
     gather_start(grad_at, s_gy, s_gx)
+    for cp in early:
+        cp.wait_send()
 
     gather_relay(grad_at, s_gy, s_gx, near[:4])
 
@@ -365,30 +382,9 @@
         g16 = gm16[0 : len(ks)].reshape(96 * len(ks), HID)
         return bdot(g16, g16, TN_DIMS)
 
-    gram = gram_of((0,) + near[:4]) + gram_of(near[4:])
-    eye = (
-        lax.broadcasted_iota(jnp.int32, (HID, HID), 0) == lax.broadcasted_iota(jnp.int32, (HID, HID), 1)
-    ).astype(F32)
-
-    norm2 = jnp.sum(jnp.sum(gram * eye, axis=0, keepdims=True), axis=1, keepdims=True)
-    root = lax.rsqrt(norm2 + EPS_NORM)
-    gram = gram * (root * root)
-
-    def times(a, b):
-        return bdot(a.astype(BF16), b)
-
-    def residue(a):
-        a16 = a.astype(BF16)
-        return (NS_B * a + NS_C * bdot(a16, a16)).astype(BF16)
-
-    q0 = residue(gram)
-    first = NS_A * gram + times(gram, q0)
-    q1 = residue(NS_A * first + times(first, q0))
-    ortho = grow[...] * root
-    ortho = NS_A * ortho + times(ortho, q0)
-    xo[c] = NS_A * ortho + times(ortho, q1)
-    s_x = sem_ids(1)
-    send(xo.at[c], xo.at[c], s_x, (sib, o))
+    drain()
+    gram = gram_of((0,) + near[:4])
+
     def put_before(block):
         rows3 = block.astype(F32)[8:32]
         for ch in range(CH):
@@ -449,6 +445,30 @@
 
     lax.fori_loop(0, CH, chunk2, 0)
 
+    gram = gram + gram_of(near[4:])
+    eye = (
+        lax.broadcasted_iota(jnp.int32, (HID, HID), 0) == lax.broadcasted_iota(jnp.int32, (HID, HID), 1)
+    ).astype(F32)
+
+    norm2 = jnp.sum(jnp.sum(gram * eye, axis=0, keepdims=True), axis=1, keepdims=True)
+    root = lax.rsqrt(norm2 + EPS_NORM)
+    gram = gram * (root * root)
+
+    def times(a, b):
+        return bdot(a.astype(BF16), b)
+
+    def residue(a):
+        a16 = a.astype(BF16)
+        return (NS_B * a + NS_C * bdot(a16, a16)).astype(BF16)
+
+    q0 = residue(gram)
+    first = NS_A * gram + times(gram, q0)
+    q1 = residue(NS_A * first + times(first, q0))
+    ortho = grow[...] * root
+    ortho = NS_A * ortho + times(ortho, q0)
+    xo[c] = NS_A * ortho + times(ortho, q1)
+    s_x = sem_ids(1)
+    send(xo.at[c], xo.at[c], s_x, (sib, o))
     branch = scatter_z_sum(bs, br, s_b)
     own_keep = jnp.where(own_live, tissue[o // 2], 0).astype(F32)
     res = feat[own_rows, :].astype(F32) + (own_keep * scale) * branch
@@ -458,7 +478,7 @@
     for m in range(2):
         muon_ref[m] = jnp.where(c == 0, xo[m, 0:12, :], xo[m, 12:24, :])
 
-    for cp in sent:
+    for cp in sent + along_z:
         cp.wait_send()
 
 

time: 65.1 us -> 64.6 us (level)
  no operation moved by 1% of the time
where the time goes in v7:
time: 64.6 us; the launch traced here: 64.4 us
  Pallas kernels  61.6 us (95%)
  local copies, waits for them, and re-layouts  2.1 us (3%)
  between operations  0.65 us (1%)
    pallas_call x1, Pallas kernels, shards(): pl.pallas_call(body, out_shape=(jax.ShapeDtypeStruct((2, OWN_TOK, D), BF1...  61.6 us
    another operation x1, local copies, waits for them, and re-layouts, shards(): tokens[1].reshape(4, 8, D)  1.47 us

profile of v7, /device:TPU:1, one launch (start us, length us, event | category | flops | bytes accessed | tf_op | source)
XLA Modules:
  0.0 64.4 jit_solution(1331424236862784093)
XLA Ops:
  0.6 61.6 %shard_map.129 = (bf16[2,32,768]{2,1,0:T(8,128)(2,1)}, f32[2,12,384]{2,1,0:T(8,128)}) custom-call(s32[64]{0:T(128)} %lens_h.1, s32[4]{0:T(128)} %bitcast.17, bf16[256,768]{1,0:T(8,128)(2,1)} %bitcast.14, bf16[256,768]{1,0:T(8,128)(2,1)} %bitcast.15, f32[7,7,768]{2,1,0:T(8,128)} %dk_h.1, f32[768]{0:T(1024)} %gain_h.1, bf16[12,384]{1,0:T(8,128)(2,1)} %wu_h.1, ...), custom_call_target="tpu_custom_call" | custom-call | tf_op jit(solution)/shard_map/pallas_call | solution.py:537
  62.3 0.0 copy-start
  62.3 1.5 %slice_bitcast_fusion = (bf16[4,8,768]{2,1,0:T(8,128)(2,1)}, bf16[4,8,768]{2,1,0:T(8,128)(2,1)}) fusion(bf16[2,32,768]{2,1,0:T(8,128)(2,1)} %get-tuple-element.6), kind=kLoop, calls=%fused_computation | loop fusion | bytes 196608 | tf_op jit(solution)/shard_map/reshape;squeeze | solution.py:564
  63.8 0.0 copy-done
  63.8 0.6 slice_bitcast_fusion.2
Async XLA Ops:
  62.3 1.5 %copy-start = (f32[2,12,384]{2,1,0:T(8,128)S(1)}, f32[2,12,384]{2,1,0:T(8,128)}, u32[]{:S(2)}) copy-start(f32[2,12,384]{2,1,0:T(8,128)} %get-tuple-element.7) | copy-start | bytes 110596

commit v8 on v7

--- a/solution.py
+++ b/solution.py
@@ -199,6 +199,8 @@
             frame[ch, 3 + 8 * q : 11 + 8 * q, 3:11, :] = f[:, 128 * ch : 128 * ch + 128].reshape(8, 8, 128)
         left[1, rows, :] = ((keep * scale) * cot[rows, :].astype(F32)).astype(BF16)
 
+    gather_relay(weight_at, s_wy, s_wx, near[:2])
+
     arrived(halo.at[0], s_halo)
     arrived(halo.at[1], s_halo + 1)
     before = jnp.where(t > 0, halo[0].astype(F32), 0.0)
@@ -225,7 +227,6 @@
 
         lax.fori_loop(0, CH, chunk, 0)
 
-    gather_relay(weight_at, s_wy, s_wx, near[:2])
     conv_half(0)
     gather_relay(weight_at, s_wy, s_wx, near[2:6])
     conv_half(1)

time: 64.6 us -> 64.6 us (level)
  no operation moved by 1% of the time
where the time goes in v8:
time: 64.6 us; the launch traced here: 64.4 us
  Pallas kernels  61.7 us (96%)
  local copies, waits for them, and re-layouts  2.1 us (3%)
  between operations  0.65 us (1%)
    pallas_call x1, Pallas kernels, shards(): pl.pallas_call(body, out_shape=(jax.ShapeDtypeStruct((2, OWN_TOK, D), BF1...  61.7 us
    another operation x1, local copies, waits for them, and re-layouts, shards(): tokens[1].reshape(4, 8, D)  1.47 us

profile of v8, /device:TPU:1, one launch (start us, length us, event | category | flops | bytes accessed | tf_op | source)
XLA Modules:
  0.0 64.4 jit_solution(369312387450603170)
XLA Ops:
  0.6 61.7 %shard_map.129 = (bf16[2,32,768]{2,1,0:T(8,128)(2,1)}, f32[2,12,384]{2,1,0:T(8,128)}) custom-call(s32[64]{0:T(128)} %lens_h.1, s32[4]{0:T(128)} %bitcast.17, bf16[256,768]{1,0:T(8,128)(2,1)} %bitcast.14, bf16[256,768]{1,0:T(8,128)(2,1)} %bitcast.15, f32[7,7,768]{2,1,0:T(8,128)} %dk_h.1, f32[768]{0:T(1024)} %gain_h.1, bf16[12,384]{1,0:T(8,128)(2,1)} %wu_h.1, ...), custom_call_target="tpu_custom_call" | custom-call | tf_op jit(solution)/shard_map/pallas_call | solution.py:538
  62.3 0.0 copy-start
  62.3 1.5 %slice_bitcast_fusion = (bf16[4,8,768]{2,1,0:T(8,128)(2,1)}, bf16[4,8,768]{2,1,0:T(8,128)(2,1)}) fusion(bf16[2,32,768]{2,1,0:T(8,128)(2,1)} %get-tuple-element.6), kind=kLoop, calls=%fused_computation | loop fusion | bytes 196608 | tf_op jit(solution)/shard_map/reshape;squeeze | solution.py:565
  63.8 0.0 copy-done
  63.8 0.6 slice_bitcast_fusion.2
Async XLA Ops:
  62.3 1.5 %copy-start = (f32[2,12,384]{2,1,0:T(8,128)S(1)}, f32[2,12,384]{2,1,0:T(8,128)}, u32[]{:S(2)}) copy-start(f32[2,12,384]{2,1,0:T(8,128)} %get-tuple-element.7) | copy-start | bytes 110596
